TPU v7x, 256 devices: a whole 4x4x8 slice. The times are simulated.
256 devices in a mesh: gx: 16 (over z, core), gy: 16 (over y, x).
Axes of the slice: x: 4, y: 4, z: 8, core: 2. Of those that a mesh axis runs over, the one named last changes fastest.
Arguments:
- fields: float32 [2, 2048, 2048], P(None, 'gy', 'gx'), may hold values from -8 to 8
- material: int32 [2048, 2048], P('gy', 'gx'), may hold values from 0 to 7
- conduct: float32 [2, 8], replicated, may hold values from 0.25 to 4
- joints_x: int32 [2048, 8], P('gy'), may hold values from 1 to 2047
- joints_y: int32 [2048, 8], P('gx'), may hold values from 1 to 2047
Outputs:
- half_step: float32 [2, 2048, 2048], P(None, 'gy', 'gx')
- advanced: float32 [2, 2048, 2048], P(None, 'gy', 'gx')
Inputs may be any that keep to these rules, and one draw needn't show every extreme that they name: `joints_x`: entries of one row may repeat. `joints_y`: entries of one column may repeat.
All inputs are finite; a program needn't handle non-finite values.
Results may differ from a plain program's by a relative error of at most 0.0015.
Values sent between devices are 32-bit elements; how exact they have to be, the bound alone decides.
No kernel may reach another device: no remote copies, remote signals or barrier semaphores. Data moves between devices by JAX's collectives and lax.ppermute only.
A program may use at most 64 MiB of HBM per device.

v0:
```python
import jax
import jax.numpy as jnp
from jax import lax
from jax.sharding import PartitionSpec as P

MATERIALS = 8
FOURIER = 8192
DRYING = 4096


def with_halo(block, sides, width):
    for axis, dim in sides:
        count = lax.axis_size(axis)
        forward = [(i, i + 1) for i in range(count - 1)]
        backward = [(target, source) for source, target in forward]
        low = lax.ppermute(
            lax.slice_in_dim(block, block.shape[dim] - width, None, axis=dim), axis, forward
        )
        high = lax.ppermute(lax.slice_in_dim(block, 0, width, axis=dim), axis, backward)
        block = jnp.concatenate([low, block, high], axis=dim)
    return block


def shifted(array_in, stride, line_axis, fill_value, earlier):
    length = array_in.shape[line_axis]
    filler = jnp.full(
        array_in.shape[:line_axis] + (stride,) + array_in.shape[line_axis + 1 :],
        fill_value,
        array_in.dtype,
    )
    if earlier:
        return jnp.concatenate(
            [filler, lax.slice_in_dim(array_in, 0, length - stride, axis=line_axis)], line_axis
        )
    return jnp.concatenate(
        [lax.slice_in_dim(array_in, stride, length, axis=line_axis), filler], line_axis
    )


def cyclic(lower, diagonal, upper, sides, line_axis):
    length = diagonal.shape[line_axis]
    for rounds in range((length - 1).bit_length()):
        stride = 1 << rounds
        before_gain = -lower / shifted(diagonal, stride, line_axis, 1.0, True)
        after_gain = -upper / shifted(diagonal, stride, line_axis, 1.0, False)
        new_diagonal = (
            diagonal
            + before_gain * shifted(upper, stride, line_axis, 0.0, True)
            + after_gain * shifted(lower, stride, line_axis, 0.0, False)
        )
        sides = tuple(
            (
                entry
                + before_gain * shifted(entry, stride, line_axis, 0.0, True)
                + after_gain * shifted(entry, stride, line_axis, 0.0, False)
                for entry in sides
            )
        )
        lower = before_gain * shifted(lower, stride, line_axis, 0.0, True)
        upper = after_gain * shifted(upper, stride, line_axis, 0.0, False)
        diagonal = new_diagonal
    return tuple((entry / diagonal for entry in sides))


def per_device(fields, material, conduct, joints_x, joints_y):
    row_count, col_count = material.shape
    conduction = jnp.zeros((2, row_count, col_count), jnp.float32)
    for klass in range(MATERIALS):
        conduction = jnp.where(
            material[None] == klass, conduct[:, klass][:, None, None], conduction
        )
    padded = with_halo(conduction, (("gx", 2), ("gy", 1)), 1)
    center = padded[:, 1:-1, 1:-1]
    col_pos = lax.axis_index("gx") * col_count + jnp.arange(col_count, dtype=jnp.int32)
    row_pos = lax.axis_index("gy") * row_count + jnp.arange(row_count, dtype=jnp.int32)
    width_total = col_count * lax.axis_size("gx")
    height_total = row_count * lax.axis_size("gy")
    face_scale = jnp.array([FOURIER, DRYING], jnp.float32)[:, None, None]
    cut_west = jnp.any(joints_x[:, None, :] == col_pos[None, :, None], axis=2).astype(jnp.float32)
    cut_east = jnp.any(joints_x[:, None, :] == col_pos[None, :, None] + 1, axis=2).astype(
        jnp.float32
    )
    cut_north = jnp.any(joints_y[None, :, :] == row_pos[:, None, None], axis=2).astype(jnp.float32)
    cut_south = jnp.any(joints_y[None, :, :] == row_pos[:, None, None] + 1, axis=2).astype(
        jnp.float32
    )
    west_face = jnp.where(
        col_pos > 0, face_scale * 0.5 * (padded[:, 1:-1, :-2] + center) * (1.0 - cut_west), 0.0
    )
    east_face = jnp.where(
        col_pos < width_total - 1,
        face_scale * 0.5 * (center + padded[:, 1:-1, 2:]) * (1.0 - cut_east),
        0.0,
    )
    north_face = jnp.where(
        row_pos[:, None] > 0,
        face_scale * 0.5 * (padded[:, :-2, 1:-1] + center) * (1.0 - cut_north),
        0.0,
    )
    south_face = jnp.where(
        row_pos[:, None] < height_total - 1,
        face_scale * 0.5 * (center + padded[:, 2:, 1:-1]) * (1.0 - cut_south),
        0.0,
    )
    values = lax.all_to_all(fields, "gx", split_axis=1, concat_axis=2, tiled=True)
    low_face = lax.all_to_all(west_face, "gx", split_axis=1, concat_axis=2, tiled=True)
    high_face = lax.all_to_all(east_face, "gx", split_axis=1, concat_axis=2, tiled=True)
    solved = cyclic(-low_face, 1.0 + low_face + high_face, -high_face, (values,), 2)[0]
    half_step = lax.all_to_all(solved, "gx", split_axis=2, concat_axis=1, tiled=True)
    values = lax.all_to_all(half_step, "gy", split_axis=2, concat_axis=1, tiled=True)
    low_face = lax.all_to_all(north_face, "gy", split_axis=2, concat_axis=1, tiled=True)
    high_face = lax.all_to_all(south_face, "gy", split_axis=2, concat_axis=1, tiled=True)
    solved = cyclic(-low_face, 1.0 + low_face + high_face, -high_face, (values,), 1)[0]
    advanced = lax.all_to_all(solved, "gy", split_axis=1, concat_axis=2, tiled=True)
    return (half_step, advanced)


def solution(mesh):
    return jax.shard_map(
        per_device,
        mesh=mesh,
        in_specs=(P(None, "gy", "gx"), P("gy", "gx"), P(), P("gy", None), P("gx", None)),
        out_specs=(P(None, "gy", "gx"), P(None, "gy", "gx")),
        check_vma=False,
    )
```

profile of v0, /device:TPU:1, one launch (start us, length us, event | category | flops | bytes accessed | tf_op | source)
XLA Modules:
  0.0 162.6 jit_solution(1300432603733610993)
XLA Ops:
  3.6 4.9 %collective-permute-start = (f32[2,128,1]{2,0,1:T(2,128)S(1)}, f32[2,128,1]{2,0,1:T(2,128)S(1)}, u32[]{:S(2)}, u32[]{:S(2)}) collective-permute-start(f32[2,128,1]{2,0,1:T(2,128)S(1)} %get-tuple-element.263), channel_id=1, source_target_pairs={{0,16},{16,32},{32,48},{48,64},{64,80},{80,96},{96,112},{112,128},... | collective-permute-start | bytes 3080 | tf_op jit(solution)/shard_map/ppermute | solution.py:16
  12.9 1.9 %collective-permute-done.1 = f32[2,128,1]{2,0,1:T(2,128)S(1)} collective-permute-done((f32[2,128,1]{2,0,1:T(2,128)S(1)}, f32[2,128,1]{2,0,1:T(2,128)S(1)}, u32[]{:S(2)}, u32[]{:S(2)}) %collective-permute-start.1) | collective-permute-done | bytes 1056 | tf_op jit(solution)/shard_map/ppermute | solution.py:19
  14.9 3.1 %collective-permute-start.2 = (f32[2,1,130]{2,0,1:T(2,128)S(1)}, f32[2,1,130]{2,0,1:T(2,128)S(1)}, u32[]{:S(2)}, u32[]{:S(2)}) collective-permute-start(f32[2,1,130]{2,0,1:T(2,128)S(1)} %get-tuple-element.82), channel_id=1, source_target_pairs={{0,1},{1,2},{2,3},{3,4},{4,5},{5,6},{6,7},{7,8},{8,9},{9,10},{10,1... | collective-permute-start | bytes 3128 | tf_op jit(solution)/shard_map/ppermute | solution.py:16
  19.4 3.0 %collective-permute-done.3 = f32[2,1,130]{2,0,1:T(2,128)S(1)} collective-permute-done((f32[2,1,130]{2,0,1:T(2,128)S(1)}, f32[2,1,130]{2,0,1:T(2,128)S(1)}, u32[]{:S(2)}, u32[]{:S(2)}) %collective-permute-start.3) | collective-permute-done | bytes 1072 | tf_op jit(solution)/shard_map/ppermute | solution.py:19
  22.4 2.4 %broadcast_select_fusion.1 = (f32[2,128,128]{2,0,1:T(2,128)S(1)}, f32[2,128,128]{2,0,1:T(2,128)S(1)}, f32[2,128,128]{2,0,1:T(2,128)}) fusion(pred[128]{0:T(512)(128)(4,1)S(1)} %get-tuple-element.278, f32[2,128,128]{2,0,1:T(2,128)S(1)} %select_select_fusion, f32[2,128,1]{2,0,1:T(2,128)S(1)} %collective-permute-done.1, ...), kind=kLoop, calls=%fused_computation.158 | loop fusion | flops 622592 | bytes 725416 | tf_op jit(solution)/shard_map/jit(_where)/select_n | solution.py:95
  25.6 8.3 %all-to-all-start.5 = ((f32[2,128,128]{1,0,2:T(2,128)}), f32[2,128,128]{1,0,2:T(2,128)S(1)}, u32[]{:S(2)}, u32[]{:S(2)}) async-start(f32[2,128,128]{1,0,2:T(2,128)} %copy.57), calls=%async_computation.5 | async-start | bytes 262144 | tf_op jit(solution)/shard_map/all_to_all | solution.py:111
  35.4 5.3 %all-to-all-done.5 = f32[2,128,128]{1,0,2:T(2,128)S(1)} async-done(((f32[2,128,128]{1,0,2:T(2,128)}), f32[2,128,128]{1,0,2:T(2,128)S(1)}, u32[]{:S(2)}, u32[]{:S(2)}) %all-to-all-start.5) | async-done | bytes 131104 | tf_op jit(solution)/shard_map/all_to_all | solution.py:111
  40.7 3.5 %all-to-all-start.6 = ((f32[2,128,128]{1,0,2:T(2,128)}), f32[2,128,128]{1,0,2:T(2,128)S(1)}, u32[]{:S(2)}, u32[]{:S(2)}) async-start(f32[2,128,128]{1,0,2:T(2,128)} %copy.59), calls=%async_computation.6 | async-start | bytes 262144 | tf_op jit(solution)/shard_map/all_to_all | solution.py:112
  45.1 6.5 %all-to-all-done.6 = f32[2,128,128]{1,0,2:T(2,128)S(1)} async-done(((f32[2,128,128]{1,0,2:T(2,128)}), f32[2,128,128]{1,0,2:T(2,128)S(1)}, u32[]{:S(2)}, u32[]{:S(2)}) %all-to-all-start.6) | async-done | bytes 131104 | tf_op jit(solution)/shard_map/all_to_all | solution.py:112
  51.6 11.5 %all-to-all-start = ((f32[2,128,128]{2,0,1:T(2,128)}), f32[2,128,128]{2,0,1:T(2,128)S(1)}, u32[]{:S(2)}, u32[]{:S(2)}) async-start(f32[2,128,128]{2,0,1:T(2,128)} %copy.47), calls=%async_computation | async-start | bytes 262144 | tf_op jit(solution)/shard_map/all_to_all | solution.py:105
  63.1 9.1 %all-to-all-done = f32[2,128,128]{2,0,1:T(2,128)S(1)} async-done(((f32[2,128,128]{2,0,1:T(2,128)}), f32[2,128,128]{2,0,1:T(2,128)S(1)}, u32[]{:S(2)}, u32[]{:S(2)}) %all-to-all-start) | async-done | bytes 131104 | tf_op jit(solution)/shard_map/all_to_all | solution.py:105
  72.3 3.4 %all-to-all-start.1 = ((f32[2,128,128]{2,0,1:T(2,128)}), f32[2,128,128]{2,0,1:T(2,128)S(1)}, u32[]{:S(2)}, u32[]{:S(2)}) async-start(f32[2,128,128]{2,0,1:T(2,128)} %fusion.12), calls=%async_computation.1 | async-start | bytes 262144 | tf_op jit(solution)/shard_map/all_to_all | solution.py:106
  75.8 8.4 %all-to-all-done.1 = f32[2,128,128]{2,0,1:T(2,128)S(1)} async-done(((f32[2,128,128]{2,0,1:T(2,128)}), f32[2,128,128]{2,0,1:T(2,128)S(1)}, u32[]{:S(2)}, u32[]{:S(2)}) %all-to-all-start.1) | async-done | bytes 131104 | tf_op jit(solution)/shard_map/all_to_all | solution.py:106
  84.1 3.4 %all-to-all-start.2 = ((f32[2,128,128]{2,0,1:T(2,128)}), f32[2,128,128]{2,0,1:T(2,128)S(1)}, u32[]{:S(2)}, u32[]{:S(2)}) async-start(f32[2,128,128]{2,0,1:T(2,128)} %get-tuple-element.84), calls=%async_computation.2 | async-start | bytes 262144 | tf_op jit(solution)/shard_map/all_to_all | solution.py:107
  87.7 9.0 %all-to-all-done.2 = f32[2,128,128]{2,0,1:T(2,128)S(1)} async-done(((f32[2,128,128]{2,0,1:T(2,128)}), f32[2,128,128]{2,0,1:T(2,128)S(1)}, u32[]{:S(2)}, u32[]{:S(2)}) %all-to-all-start.2) | async-done | bytes 131104 | tf_op jit(solution)/shard_map/all_to_all | solution.py:107
  103.9 4.0 %reshape.78 = f32[16,1,2048]{2,1,0:T(1,128)} reshape(f32[2048,2,8]{2,1,0:T(2,128)S(1)} %bitcast.95) | data formatting | bytes 262144
  107.9 3.6 %all-to-all-start.3 = ((f32[16,1,2048]{2,1,0:T(1,128)}), f32[16,1,2048]{2,1,0:T(1,128)S(1)}, u32[]{:S(2)}, u32[]{:S(2)}) async-start(f32[16,1,2048]{2,1,0:T(1,128)} %reshape.78), calls=%async_computation.3 | async-start | bytes 262144 | tf_op jit(solution)/shard_map/all_to_all | solution.py:109
  111.6 8.3 %all-to-all-done.3 = f32[16,1,2048]{2,1,0:T(1,128)S(1)} async-done(((f32[16,1,2048]{2,1,0:T(1,128)}), f32[16,1,2048]{2,1,0:T(1,128)S(1)}, u32[]{:S(2)}, u32[]{:S(2)}) %all-to-all-start.3) | async-done | bytes 131104 | tf_op jit(solution)/shard_map/all_to_all | solution.py:109
  121.3 3.2 %reshape.79 = f32[2048,2,8]{2,1,0:T(2,128)S(1)} reshape(f32[16,2048]{1,0:T(8,128)S(1)} %reduce.16) | data formatting | bytes 262144
  126.1 3.5 %all-to-all-start.4 = ((f32[2,128,128]{1,0,2:T(2,128)}), f32[2,128,128]{1,0,2:T(2,128)S(1)}, u32[]{:S(2)}, u32[]{:S(2)}) async-start(f32[2,128,128]{1,0,2:T(2,128)} %copy.55), calls=%async_computation.4 | async-start | bytes 262144 | tf_op jit(solution)/shard_map/all_to_all | solution.py:110
  129.7 7.2 %all-to-all-done.4 = f32[2,128,128]{1,0,2:T(2,128)S(1)} async-done(((f32[2,128,128]{1,0,2:T(2,128)}), f32[2,128,128]{1,0,2:T(2,128)S(1)}, u32[]{:S(2)}, u32[]{:S(2)}) %all-to-all-start.4) | async-done | bytes 131104 | tf_op jit(solution)/shard_map/all_to_all | solution.py:110
  144.0 3.3 %reshape.80 = f32[16,1,2048]{2,1,0:T(1,128)S(1)} reshape(f32[2048,2,8]{2,1,0:T(2,128)S(1)} %bitcast.97) | data formatting | bytes 262144
  147.3 9.6 %all_to_all.144 = f32[16,1,2048]{2,1,0:T(1,128)S(1)} all-to-all(f32[16,1,2048]{2,1,0:T(1,128)S(1)} %reshape.80), channel_id=1, replica_groups=mesh['gx'=16,'gy'=16] {'gy'}, dimensions={0} | all-to-all | bytes 262144 | tf_op jit(solution)/shard_map/all_to_all | solution.py:114
  157.8 3.2 %reshape.81 = f32[2048,2,8]{2,1,0:T(2,128)S(1)} reshape(f32[16,2048]{1,0:T(8,128)S(1)} %reduce.17) | data formatting | bytes 262144
  (172 shorter events, 31.1 us)
Async XLA Ops:
  0.6 33.3 %copy-start.1 = (f32[2,128,128]{2,1,0:T(8,128)S(1)}, f32[2,128,128]{2,1,0:T(8,128)}, u32[]{:S(2)}) copy-start(f32[2,128,128]{2,1,0:T(8,128)} %param.6) | copy-start | bytes 393220
  1.6 42.6 %copy-start.2 = (f32[2]{0:T(128)S(1)}, f32[2]{0:T(128)}, u32[]{:S(2)}) copy-start(f32[2]{0:T(128)} %constant.432) | copy-start | bytes 28
  3.6 9.3 %collective-permute-start = (f32[2,128,1]{2,0,1:T(2,128)S(1)}, f32[2,128,1]{2,0,1:T(2,128)S(1)}, u32[]{:S(2)}, u32[]{:S(2)}) collective-permute-start(f32[2,128,1]{2,0,1:T(2,128)S(1)} %get-tuple-element.263), channel_id=1, source_target_pairs={{0,16},{16,32},{32,48},{48,64},{64,80},{80,96},{96,112},{112,128},... | collective-permute-start | bytes 3080 | tf_op jit(solution)/shard_map/ppermute | solution.py:16
  8.6 6.3 %collective-permute-start.1 = (f32[2,128,1]{2,0,1:T(2,128)S(1)}, f32[2,128,1]{2,0,1:T(2,128)S(1)}, u32[]{:S(2)}, u32[]{:S(2)}) collective-permute-start(f32[2,128,1]{2,0,1:T(2,128)S(1)} %get-tuple-element.264), channel_id=1, source_target_pairs={{16,0},{32,16},{48,32},{64,48},{80,64},{96,80},{112,96},{128,112},... | collective-permute-start | bytes 3080 | tf_op jit(solution)/shard_map/ppermute | solution.py:19
  14.9 4.4 %collective-permute-start.2 = (f32[2,1,130]{2,0,1:T(2,128)S(1)}, f32[2,1,130]{2,0,1:T(2,128)S(1)}, u32[]{:S(2)}, u32[]{:S(2)}) collective-permute-start(f32[2,1,130]{2,0,1:T(2,128)S(1)} %get-tuple-element.82), channel_id=1, source_target_pairs={{0,1},{1,2},{2,3},{3,4},{4,5},{5,6},{6,7},{7,8},{8,9},{9,10},{10,1... | collective-permute-start | bytes 3128 | tf_op jit(solution)/shard_map/ppermute | solution.py:16
  18.0 4.3 %collective-permute-start.3 = (f32[2,1,130]{2,0,1:T(2,128)S(1)}, f32[2,1,130]{2,0,1:T(2,128)S(1)}, u32[]{:S(2)}, u32[]{:S(2)}) collective-permute-start(f32[2,1,130]{2,0,1:T(2,128)S(1)} %get-tuple-element.83), channel_id=1, source_target_pairs={{1,0},{2,1},{3,2},{4,3},{5,4},{6,5},{7,6},{8,7},{9,8},{10,9},{11,1... | collective-permute-start | bytes 3128 | tf_op jit(solution)/shard_map/ppermute | solution.py:19
  25.6 15.2 %all-to-all-start.5 = ((f32[2,128,128]{1,0,2:T(2,128)}), f32[2,128,128]{1,0,2:T(2,128)S(1)}, u32[]{:S(2)}, u32[]{:S(2)}) async-start(f32[2,128,128]{1,0,2:T(2,128)} %copy.57), calls=%async_computation.5 | async-start | bytes 262144 | tf_op jit(solution)/shard_map/all_to_all | solution.py:111
  40.7 10.9 %all-to-all-start.6 = ((f32[2,128,128]{1,0,2:T(2,128)}), f32[2,128,128]{1,0,2:T(2,128)S(1)}, u32[]{:S(2)}, u32[]{:S(2)}) async-start(f32[2,128,128]{1,0,2:T(2,128)} %copy.59), calls=%async_computation.6 | async-start | bytes 262144 | tf_op jit(solution)/shard_map/all_to_all | solution.py:112
  51.6 20.6 %all-to-all-start = ((f32[2,128,128]{2,0,1:T(2,128)}), f32[2,128,128]{2,0,1:T(2,128)S(1)}, u32[]{:S(2)}, u32[]{:S(2)}) async-start(f32[2,128,128]{2,0,1:T(2,128)} %copy.47), calls=%async_computation | async-start | bytes 262144 | tf_op jit(solution)/shard_map/all_to_all | solution.py:105
  72.3 11.9 %all-to-all-start.1 = ((f32[2,128,128]{2,0,1:T(2,128)}), f32[2,128,128]{2,0,1:T(2,128)S(1)}, u32[]{:S(2)}, u32[]{:S(2)}) async-start(f32[2,128,128]{2,0,1:T(2,128)} %fusion.12), calls=%async_computation.1 | async-start | bytes 262144 | tf_op jit(solution)/shard_map/all_to_all | solution.py:106
  84.1 12.5 %all-to-all-start.2 = ((f32[2,128,128]{2,0,1:T(2,128)}), f32[2,128,128]{2,0,1:T(2,128)S(1)}, u32[]{:S(2)}, u32[]{:S(2)}) async-start(f32[2,128,128]{2,0,1:T(2,128)} %get-tuple-element.84), calls=%async_computation.2 | async-start | bytes 262144 | tf_op jit(solution)/shard_map/all_to_all | solution.py:107
  107.9 12.0 %all-to-all-start.3 = ((f32[16,1,2048]{2,1,0:T(1,128)}), f32[16,1,2048]{2,1,0:T(1,128)S(1)}, u32[]{:S(2)}, u32[]{:S(2)}) async-start(f32[16,1,2048]{2,1,0:T(1,128)} %reshape.78), calls=%async_computation.3 | async-start | bytes 262144 | tf_op jit(solution)/shard_map/all_to_all | solution.py:109
  125.3 12.1 %copy-start = (f32[2,8,16,128]{3,1,2,0:T(8,128)}, f32[2,8,16,128]{3,1,2,0:T(8,128)S(1)}, u32[]{:S(2)}) copy-start(f32[2,8,16,128]{3,1,2,0:T(8,128)S(1)} %copy.65) | copy-start | bytes 393220
  126.1 10.8 %all-to-all-start.4 = ((f32[2,128,128]{1,0,2:T(2,128)}), f32[2,128,128]{1,0,2:T(2,128)S(1)}, u32[]{:S(2)}, u32[]{:S(2)}) async-start(f32[2,128,128]{1,0,2:T(2,128)} %copy.55), calls=%async_computation.4 | async-start | bytes 262144 | tf_op jit(solution)/shard_map/all_to_all | solution.py:110
where the time goes:
time: 164 us; the launch traced here: 163 us
  waiting for transfers between devices  58.7 us (36%)
  starting transfers between devices  48.5 us (30%)
  local copies, waits for them, and re-layouts  29.7 us (18%)
  other arithmetic  14.3 us (9%)
  blocking collectives  9.58 us (6%)
  between operations  1.89 us (1%)
    unnamed x13, local copies, waits for them, and re-layouts  16 us
    all_to_all x1, starting transfers between devices, per_device(): lax.all_to_all(fields, 'gx', split_axis=1, concat_axis=2, tiled=True)  11.5 us
    all_to_all x1, blocking collectives, per_device(): lax.all_to_all(solved, 'gy', split_axis=1, concat_axis=2, tiled=True)  9.58 us
    all_to_all x1, waiting for transfers between devices, per_device(): lax.all_to_all(fields, 'gx', split_axis=1, concat_axis=2, tiled=True)  9.13 us
    all_to_all x1, waiting for transfers between devices, per_device(): lax.all_to_all(east_face, 'gx', split_axis=1, concat_axis=2, tiled=True)  8.98 us
    all_to_all x1, waiting for transfers between devices, per_device(): lax.all_to_all(west_face, 'gx', split_axis=1, concat_axis=2, tiled=True)  8.35 us
    all_to_all x1, starting transfers between devices, per_device(): lax.all_to_all(north_face, 'gy', split_axis=2, concat_axis=1, tiled=True)  8.31 us
    all_to_all x1, waiting for transfers between devices, per_device(): lax.all_to_all(solved, 'gx', split_axis=2, concat_axis=1, tiled=True)  8.3 us
  transfers between devices with their start and end apart: 11, of which 9 were waited for; matrix products, arithmetic and copies ran while one was open for 3% of the time, Pallas kernels for 0%

commit v1 on v0

v1 whole, which is shorter than its diff:
```python
import jax
import jax.numpy as jnp
from jax import lax
from jax.experimental import pallas as pl
from jax.experimental.pallas import tpu as pltpu
from jax.sharding import PartitionSpec as P

MATERIALS = 8
FOURIER = 8192
DRYING = 4096
HALF_SCALE = (FOURIER * 0.5, DRYING * 0.5)

CHUNKS = 8
DEPTH = 16
SIDE = 128
DEVICES = 16
ROWS = 16

G_LOW, G_HIGH, LINK, S_LOW, S_HIGH, C_LOW, C_HIGH, OPEN = range(8)


def sublane():
    return lax.broadcasted_iota(jnp.int32, (CHUNKS, SIDE), 0)


def rolled(x, shift):
    return pltpu.roll(x, shift % CHUNKS, 0)


def conductivities(load, conduct_ref):
    out = ([], [])
    for k in range(DEPTH):
        m = load(k)
        bits = [(m & b) != 0 for b in (1, 2, 4)]
        for c in range(2):
            values = [conduct_ref[c, q] * HALF_SCALE[c] for q in range(MATERIALS)]
            for bit in bits:
                values = [
                    jnp.where(bit, values[i + 1], values[i]) for i in range(0, len(values), 2)
                ]
            out[c].append(values[0])
    return out


def cut_bits(joints_ref, base):
    lane_joints = joints_ref[...] - base
    chunk_start = sublane() * DEPTH
    flags = jnp.zeros((CHUNKS, SIDE), jnp.int32)
    for q in range(joints_ref.shape[0]):
        place = jnp.broadcast_to(lane_joints[q : q + 1, :], (CHUNKS, SIDE)) - chunk_start
        inside = (place >= 0) & (place < DEPTH)
        flags = flags | jnp.where(inside, jnp.left_shift(1, place & (DEPTH - 1)), 0)
    return flags


def face_links(cells, flags):
    links = []
    for k in range(DEPTH):
        before = rolled(cells[DEPTH - 1], 1) if k == 0 else cells[k - 1]
        links.append(jnp.where((flags & (1 << k)) != 0, 0.0, before + cells[k]))
    return links


ORDER = [
    (m, m - half, m + half)
    for half in (1, 2, 4, 8)
    for m in range(half - 1, DEPTH - 1, 2 * half)
]


def factor_chunk(links):
    first = sublane() == 0
    ground = {k: jnp.ones((CHUNKS, SIDE), jnp.float32) for k in range(DEPTH)}
    ground[-1] = jnp.zeros((CHUNKS, SIDE), jnp.float32)
    below = {k: links[k] for k in range(DEPTH)}
    factors = []
    for m, low, high in ORDER:
        a, b, g = below[m], below[high], ground[m]
        inverse = 1.0 / (a + b + g)
        if m == 0:
            inverse = jnp.where(first, 0.0, inverse)
        to_low, to_high = a * inverse, b * inverse
        if m == 0:
            to_low = jnp.where(first, 1.0, to_low)
        ground[low] = ground[low] + to_low * g
        ground[high] = ground[high] + to_high * g
        below[high] = to_low * b
        factors.append((to_low, to_high, inverse))
    return factors, (ground[-1], ground[DEPTH - 1], below[DEPTH - 1])


def source_chunk(factors, sources):
    source = dict(enumerate(sources))
    source[-1] = jnp.zeros((CHUNKS, SIDE), jnp.float32)
    offsets = []
    for (m, low, high), (to_low, to_high, inverse) in zip(ORDER, factors):
        s = source[m]
        source[low] = source[low] + to_low * s
        source[high] = source[high] + to_high * s
        offsets.append(inverse * s)
    return offsets, (source[-1], source[DEPTH - 1])


def join_factor(a, b):
    ground = a[1] + b[0]
    inverse = 1.0 / (a[2] + b[2] + ground)
    to_low, to_high = a[2] * inverse, b[2] * inverse
    joined = (a[0] + to_low * ground, b[1] + to_high * ground, to_low * b[2])
    return (to_low, to_high, inverse), joined


def join_source(factor, a, b):
    to_low, to_high, inverse = factor
    s = a[1] + b[0]
    return inverse * s, (a[0] + to_low * s, b[1] + to_high * s)


def factor_tree(element):
    factors = []
    for step in (1, 2, 4):
        factor, element = join_factor(element, [rolled(x, -step) for x in element])
        factors.append(factor)
    return factors, element


def source_tree(factors, source):
    offsets = []
    for step, factor in zip((1, 2, 4), factors):
        offset, source = join_source(factor, source, [rolled(x, -step) for x in source])
        offsets.append(offset)
    return offsets, source


def solve_tree(factors, offsets, low, high):
    row = sublane()
    for step, (to_low, to_high, _), offset in reversed(list(zip((1, 2, 4), factors, offsets))):
        middle = offset + to_low * low + to_high * high
        upper = (row & step) != 0
        low, high = jnp.where(upper, rolled(middle, step), low), jnp.where(
            upper, rolled(high, step), middle
        )
    return low, high


def solve_chunk(factors, offsets, low, high):
    h = {-1: low, DEPTH - 1: high}
    for (m, lo, hi), (to_low, to_high, _), offset in reversed(list(zip(ORDER, factors, offsets))):
        h[m] = offset + to_low * h[lo] + to_high * h[hi]
    return [h[k] for k in range(DEPTH)]


def outer_ends(gathered_ref, ring_ref, me):
    for d in range(DEVICES):
        ring_ref[d * ROWS : (d + 1) * ROWS, :] = gathered_ref[lax.rem(me + 1 + d, DEVICES)]
    own = sublane() == CHUNKS - 1
    ends = []
    for c in range(2):

        def part(q, odd):
            return ring_ref[pl.ds(odd * ROWS + 8 * c + q, 8, stride=2 * ROWS), :]

        def gate(odd):
            return ring_ref[pl.ds(odd * ROWS + OPEN, 8, stride=2 * ROWS), :]

        elements, sources = [], []
        for odd in range(2):
            before = part(C_HIGH, 0) if odd else rolled(part(C_HIGH, 1), 1)
            entry = (before + part(C_LOW, odd)) * gate(odd)
            zero = jnp.zeros_like(entry)
            factor, element = join_factor(
                (zero, zero, entry), [part(q, odd) for q in (G_LOW, G_HIGH, LINK)]
            )
            _, source = join_source(factor, (zero, zero), [part(q, odd) for q in (S_LOW, S_HIGH)])
            if odd:
                element = [
                    jnp.where(own, y, x) for x, y in zip(element, (zero, zero, entry))
                ]
                source = [jnp.where(own, 0.0, x) for x in source]
            elements.append(element)
            sources.append(source)
        factor, element = join_factor(*elements)
        _, source = join_source(factor, *sources)
        factors, element = factor_tree(element)
        _, source = source_tree(factors, source)

        def mine(q):
            at = (DEVICES - 1) * ROWS + 8 * c + q
            return ring_ref[at : at + 1, :]

        g_low = mine(G_LOW) + element[1][0:1, :]
        g_high = mine(G_HIGH) + element[0][0:1, :]
        link = mine(LINK) + element[2][0:1, :]
        s_low = mine(S_LOW) + source[1][0:1, :]
        s_high = mine(S_HIGH) + source[0][0:1, :]
        inverse = 1.0 / (g_low * g_high + link * (g_low + g_high))
        low = (s_low * (g_high + link) + link * s_high) * inverse
        high = (s_high * (g_low + link) + link * s_low) * inverse
        ends.append(
            (jnp.broadcast_to(low, (CHUNKS, SIDE)), jnp.broadcast_to(high, (CHUNKS, SIDE)))
        )
    return ends


def save(ref, c, at, values):
    for i, x in enumerate(values):
        ref[c, at + i] = x


def load_factors(ref, c, count, at=0):
    return [tuple(ref[c, at + 3 * i + j] for j in range(3)) for i in range(count)]


CELLS = len(ORDER)
STORED = 3 * CELLS + 9
OFFSETS = CELLS + 3


def flatten(factors):
    return [x for factor in factors for x in factor]


def static_rows(pay_ref, c, element, cells, flags, is_first):
    for q, x in zip((G_LOW, G_HIGH, LINK), element):
        pay_ref[8 * c + q : 8 * c + q + 1, :] = x[0:1, :]
    pay_ref[8 * c + C_LOW : 8 * c + C_LOW + 1, :] = cells[0][0:1, :]
    pay_ref[8 * c + C_HIGH : 8 * c + C_HIGH + 1, :] = cells[DEPTH - 1][CHUNKS - 1 : CHUNKS, :]
    shut = ((flags[0:1, :] & 1) != 0) | is_first
    pay_ref[8 * c + OPEN : 8 * c + OPEN + 1, :] = jnp.where(shut, 0.0, 1.0)


def source_rows(pay_ref, c, source):
    for q, x in zip((S_LOW, S_HIGH), source):
        pay_ref[8 * c + q : 8 * c + q + 1, :] = x[0:1, :]


def spread(pay_ref, out_ref):
    pay = pay_ref[...]
    for d in range(DEVICES):
        out_ref[d] = pay


def reduce_kernel(
    fields_ref, material_ref, conduct_ref, joints_x_ref, joints_y_ref,
    out_ref, x_factor_ref, x_offset_ref, y_factor_ref, y_pay_ref,
    turned_ref, kind_ref, pay_ref,
):
    at_x, at_y = lax.axis_index("gx"), lax.axis_index("gy")
    kind_ref[...] = material_ref[...].T
    for c in range(2):
        turned_ref[c] = fields_ref[c].T
    flags = cut_bits(joints_x_ref, at_x * SIDE)
    cells = conductivities(lambda k: kind_ref[pl.ds(k, CHUNKS, stride=DEPTH), :], conduct_ref)
    for c in range(2):
        factors, element = factor_chunk(face_links(cells[c], flags))
        sources = [turned_ref[c, pl.ds(k, CHUNKS, stride=DEPTH), :] for k in range(DEPTH)]
        offsets, source = source_chunk(factors, sources)
        tree, element = factor_tree(element)
        tree_offsets, source = source_tree(tree, source)
        save(x_factor_ref, c, 0, flatten(factors + tree))
        save(x_offset_ref, c, 0, offsets + tree_offsets)
        static_rows(pay_ref, c, element, cells[c], flags, at_x == 0)
        source_rows(pay_ref, c, source)
    spread(pay_ref, out_ref)
    flags = cut_bits(joints_y_ref, at_y * SIDE)
    cells = conductivities(lambda k: material_ref[pl.ds(k, CHUNKS, stride=DEPTH), :], conduct_ref)
    y_pay_ref[...] = jnp.zeros_like(y_pay_ref)
    for c in range(2):
        factors, element = factor_chunk(face_links(cells[c], flags))
        tree, element = factor_tree(element)
        save(y_factor_ref, c, 0, flatten(factors + tree))
        static_rows(y_pay_ref, c, element, cells[c], flags, at_y == 0)


def turn_kernel(
    gathered_ref, x_factor_ref, x_offset_ref, y_factor_ref, y_pay_ref,
    half_ref, out_ref, y_offset_ref,
    ring_ref, turned_ref, pay_ref,
):
    ends = outer_ends(gathered_ref, ring_ref, lax.axis_index("gx"))
    pay_ref[...] = y_pay_ref[...]
    for c in range(2):
        factors = load_factors(x_factor_ref, c, CELLS)
        tree = load_factors(x_factor_ref, c, 3, 3 * CELLS)
        offsets = [x_offset_ref[c, i] for i in range(OFFSETS)]
        low, high = solve_tree(tree, offsets[CELLS:], *ends[c])
        for k, h in enumerate(solve_chunk(factors, offsets[:CELLS], low, high)):
            turned_ref[c, pl.ds(k, CHUNKS, stride=DEPTH), :] = h
        half_ref[c] = turned_ref[c].T
    for c in range(2):
        factors = load_factors(y_factor_ref, c, CELLS)
        tree = load_factors(y_factor_ref, c, 3, 3 * CELLS)
        sources = [half_ref[c, pl.ds(k, CHUNKS, stride=DEPTH), :] for k in range(DEPTH)]
        offsets, source = source_chunk(factors, sources)
        tree_offsets, source = source_tree(tree, source)
        save(y_offset_ref, c, 0, offsets + tree_offsets)
        source_rows(pay_ref, c, source)
    spread(pay_ref, out_ref)


def finish_kernel(gathered_ref, y_factor_ref, y_offset_ref, advanced_ref, ring_ref):
    ends = outer_ends(gathered_ref, ring_ref, lax.axis_index("gy"))
    for c in range(2):
        factors = load_factors(y_factor_ref, c, CELLS)
        tree = load_factors(y_factor_ref, c, 3, 3 * CELLS)
        offsets = [y_offset_ref[c, i] for i in range(OFFSETS)]
        low, high = solve_tree(tree, offsets[CELLS:], *ends[c])
        for k, h in enumerate(solve_chunk(factors, offsets[:CELLS], low, high)):
            advanced_ref[c, pl.ds(k, CHUNKS, stride=DEPTH), :] = h


def f32(*shape):
    return jax.ShapeDtypeStruct(shape, jnp.float32)


VMEM = pl.BlockSpec(memory_space=pltpu.VMEM)
SMEM = pl.BlockSpec(memory_space=pltpu.SMEM)
SPREAD = (DEVICES, ROWS, SIDE)
BLOCK = (2, SIDE, SIDE)
FACTORS = (2, STORED, CHUNKS, SIDE)
OFFSET = (2, OFFSETS, CHUNKS, SIDE)


def per_device(fields, material, conduct, joints_x, joints_y):
    with jax.named_scope("reduce_x"):
        pay, x_factor, x_offset, y_factor, y_pay = pl.pallas_call(
            reduce_kernel,
            out_shape=(f32(*SPREAD), f32(*FACTORS), f32(*OFFSET), f32(*FACTORS), f32(ROWS, SIDE)),
            in_specs=[VMEM, VMEM, SMEM, VMEM, VMEM],
            out_specs=(VMEM,) * 5,
            scratch_shapes=[
                pltpu.VMEM(BLOCK, jnp.float32),
                pltpu.VMEM((SIDE, SIDE), jnp.int32),
                pltpu.VMEM((ROWS, SIDE), jnp.float32),
            ],
        )(fields, material, conduct, joints_x.T, joints_y.T)
    with jax.named_scope("exchange_x"):
        gathered = lax.all_to_all(pay, "gx", 0, 0)
    with jax.named_scope("solve_x_reduce_y"):
        half_step, pay, y_offset = pl.pallas_call(
            turn_kernel,
            out_shape=(f32(*BLOCK), f32(*SPREAD), f32(*OFFSET)),
            in_specs=[VMEM] * 5,
            out_specs=(VMEM,) * 3,
            scratch_shapes=[
                pltpu.VMEM((DEVICES * ROWS, SIDE), jnp.float32),
                pltpu.VMEM(BLOCK, jnp.float32),
                pltpu.VMEM((ROWS, SIDE), jnp.float32),
            ],
        )(gathered, x_factor, x_offset, y_factor, y_pay)
    with jax.named_scope("exchange_y"):
        gathered = lax.all_to_all(pay, "gy", 0, 0)
    with jax.named_scope("solve_y"):
        advanced = pl.pallas_call(
            finish_kernel,
            out_shape=f32(*BLOCK),
            in_specs=[VMEM] * 3,
            out_specs=VMEM,
            scratch_shapes=[pltpu.VMEM((DEVICES * ROWS, SIDE), jnp.float32)],
        )(gathered, y_factor, y_offset)
    return (half_step, advanced)


def solution(mesh):
    return jax.shard_map(
        per_device,
        mesh=mesh,
        in_specs=(P(None, "gy", "gx"), P("gy", "gx"), P(), P("gy", None), P("gx", None)),
        out_specs=(P(None, "gy", "gx"), P(None, "gy", "gx")),
        check_vma=False,
    )
```

time: 164 us -> 41 us (0.25)
  waiting for transfers between devices: 58.7 us -> 0 us
  starting transfers between devices: 48.5 us -> 0 us
  local copies, waits for them, and re-layouts: 29.7 us -> 0 us
  blocking collectives: 9.58 us -> 33.5 us
  other arithmetic: 14.3 us -> 0 us
  Pallas kernels: 0 us -> 6.59 us
    all_to_all x7 -> x0, waiting for transfers between devices: 53.8 us -> none  [the longest x1 9.13 us: per_device(): lax.all_to_all(fields, 'gx', split_axis=1, concat_axis=2, tiled=True)]
    all_to_all x7 -> x0, starting transfers between devices: 37.2 us -> none  [the longest x1 11.5 us: per_device(): lax.all_to_all(fields, 'gx', split_axis=1, concat_axis=2, tiled=True)]
    all_to_all x1 -> x2, blocking collectives: 9.58 us -> 33.5 us  [the longest x1 19.2 us: per_device(): gathered = lax.all_to_all(pay, 'gx', 0, 0)]
    unnamed x13 -> x0, local copies, waits for them, and re-layouts: 16 us -> none
    ppermute x4 -> x0, starting transfers between devices: 11.3 us -> none  [the longest x2 8.04 us: with_halo(): lax.ppermute(lax.slice_in_dim(block, block.shape[dim] - width, None, axis...]
    slice x90 -> x0, local copies, waits for them, and re-layouts: 7.15 us -> none  [the longest x44 2.86 us: shifted(): lax.slice_in_dim(array_in, stride, length, axis=line_axis)]
    pallas_call x0 -> x3, Pallas kernels: none -> 6.59 us  [the longest x1 2.33 us: per_device(): pl.pallas_call(reduce_kernel, out_shape=(f32(*SPREAD), f32(*FACTORS), f32...]
    add x38 -> x0, other arithmetic: 5.59 us -> none  [the longest x18 3.24 us: cyclic(): entry + before_gain * shifted(entry, stride, line_axis, 0.0, True)]
  transfers between devices with their start and end apart: 11 -> 0, of which waited for: 9 -> 0; matrix products, arithmetic and copies ran while one was open for 3% -> 0% of each run, Pallas kernels for 0% -> 0%
where the time goes in v1:
time: 41 us; the launch traced here: 40.7 us
  blocking collectives  33.5 us (82%)
  Pallas kernels  6.59 us (16%)
  between operations  0.63 us (2%)
    all_to_all x1, blocking collectives, per_device(): gathered = lax.all_to_all(pay, 'gx', 0, 0)  19.2 us
    all_to_all x1, blocking collectives, per_device(): gathered = lax.all_to_all(pay, 'gy', 0, 0)  14.2 us
    pallas_call x1, Pallas kernels, per_device(): pl.pallas_call(reduce_kernel, out_shape=(f32(*SPREAD), f32(*FACTORS), f32...  2.33 us
    pallas_call x1, Pallas kernels, per_device(): pl.pallas_call(turn_kernel, out_shape=(f32(*BLOCK), f32(*SPREAD), f32(*OF...  2.3 us
    pallas_call x1, Pallas kernels, per_device(): pl.pallas_call(finish_kernel, out_shape=f32(*BLOCK), in_specs=[VMEM] * 3,...  1.97 us

profile of v1, /device:TPU:1, one launch (start us, length us, event | category | flops | bytes accessed | tf_op | source)
XLA Modules:
  0.0 40.7 jit_solution(9755808671759525711)
XLA Ops:
  0.6 2.3 %reduce_x.1 = (f32[16,16,128]{2,1,0:T(8,128)}, f32[2,54,8,128]{3,2,1,0:T(8,128)}, f32[2,18,8,128]{3,2,1,0:T(8,128)}, f32[2,54,8,128]{3,2,1,0:T(8,128)}, f32[16,128]{1,0:T(8,128)}) custom-call(f32[2,128,128]{2,1,0:T(8,128)} %fields_ref.1, s32[128,128]{1,0:T(8,128)} %material_ref.1, f32[2,8]{1,0:T(2,128)} %conduct_ref.1, s32[8,128]{1,0:T(8,128)} %bitcast.2, ...), custom_call_target="tpu_custom_call" | custom-call | tf_op jit(solution)/shard_map/reduce_x/pallas_call | solution.py:325
  3.0 19.2 %all_to_all.10.gathered_ref = f32[16,16,128]{2,1,0:T(8,128)} all-to-all(f32[16,16,128]{2,1,0:T(8,128)} %get-tuple-element.10), channel_id=1, replica_groups=mesh['gx'=16,'gy'=16] {'gx'}, dimensions={0} | all-to-all | bytes 262144 | tf_op jit(solution)/shard_map/exchange_x/all_to_all | solution.py:337
  22.2 2.3 %solve_x_reduce_y.1 = (f32[2,128,128]{2,1,0:T(8,128)}, f32[16,16,128]{2,1,0:T(8,128)}, f32[2,18,8,128]{3,2,1,0:T(8,128)}) custom-call(f32[16,16,128]{2,1,0:T(8,128)} %all_to_all.10.gathered_ref, f32[2,54,8,128]{3,2,1,0:T(8,128)} %get-tuple-element.11.x_factor_ref, f32[2,18,8,128]{3,2,1,0:T(8,128)} %get-tuple-element.12.x_offset_ref, ...), custom_call_target="tpu_custom_call" | custom-call | tf_op jit(solution)/shard_map/solve_x_reduce_y/pallas_call | solution.py:339
  24.5 14.2 %all_to_all.11.gathered_ref = f32[16,16,128]{2,1,0:T(8,128)} all-to-all(f32[16,16,128]{2,1,0:T(8,128)} %get-tuple-element.16), channel_id=1, replica_groups=mesh['gx'=16,'gy'=16] {'gy'}, dimensions={0} | all-to-all | bytes 262144 | tf_op jit(solution)/shard_map/exchange_y/all_to_all | solution.py:351
  38.8 2.0 %solve_y.1 = f32[2,128,128]{2,1,0:T(8,128)} custom-call(f32[16,16,128]{2,1,0:T(8,128)} %all_to_all.11.gathered_ref, f32[2,54,8,128]{3,2,1,0:T(8,128)} %get-tuple-element.13.y_factor_ref, f32[2,18,8,128]{3,2,1,0:T(8,128)} %get-tuple-element.17.y_offset_ref), custom_call_target="tpu_custom_call" | custom-call | tf_op jit(solution)/shard_map/solve_y/pallas_call | solution.py:353

commit v2 on v1

--- a/solution.py
+++ b/solution.py
@@ -240,11 +240,28 @@
 
 
 def reduce_kernel(
+    fields_in, material_in, conduct_in, joints_x_in, joints_y_in,
+    out_ref, x_factor_ref, x_offset_ref, y_factor_ref, y_pay_ref,
     fields_ref, material_ref, conduct_ref, joints_x_ref, joints_y_ref,
-    out_ref, x_factor_ref, x_offset_ref, y_factor_ref, y_pay_ref,
-    turned_ref, kind_ref, pay_ref,
+    turned_ref, kind_ref, pay_ref, sems,
 ):
     at_x, at_y = lax.axis_index("gx"), lax.axis_index("gy")
+    copies = [
+        pltpu.make_async_copy(source, target, sems.at[i])
+        for i, (source, target) in enumerate(
+            (
+                (material_in, material_ref),
+                (conduct_in, conduct_ref),
+                (joints_x_in, joints_x_ref),
+                (joints_y_in, joints_y_ref),
+                (fields_in, fields_ref),
+            )
+        )
+    ]
+    for copy in copies:
+        copy.start()
+    for copy in copies:
+        copy.wait()
     kind_ref[...] = material_ref[...].T
     for c in range(2):
         turned_ref[c] = fields_ref[c].T
@@ -297,7 +314,13 @@
     spread(pay_ref, out_ref)
 
 
-def finish_kernel(gathered_ref, y_factor_ref, y_offset_ref, advanced_ref, ring_ref):
+def finish_kernel(
+    gathered_ref, y_factor_ref, y_offset_ref, half_ref,
+    half_out, advanced_out,
+    ring_ref, advanced_ref, sems,
+):
+    copies = [pltpu.make_async_copy(half_ref, half_out, sems.at[2])]
+    copies[0].start()
     ends = outer_ends(gathered_ref, ring_ref, lax.axis_index("gy"))
     for c in range(2):
         factors = load_factors(y_factor_ref, c, CELLS)
@@ -306,6 +329,10 @@
         low, high = solve_tree(tree, offsets[CELLS:], *ends[c])
         for k, h in enumerate(solve_chunk(factors, offsets[:CELLS], low, high)):
             advanced_ref[c, pl.ds(k, CHUNKS, stride=DEPTH), :] = h
+        copies.append(pltpu.make_async_copy(advanced_ref.at[c], advanced_out.at[c], sems.at[c]))
+        copies[-1].start()
+    for copy in copies:
+        copy.wait()
 
 
 def f32(*shape):
@@ -313,30 +340,39 @@
 
 
 VMEM = pl.BlockSpec(memory_space=pltpu.VMEM)
-SMEM = pl.BlockSpec(memory_space=pltpu.SMEM)
+HBM = pl.BlockSpec(memory_space=pltpu.HBM)
 SPREAD = (DEVICES, ROWS, SIDE)
+PARAMS = pltpu.CompilerParams(vmem_limit_bytes=8 << 20)
 BLOCK = (2, SIDE, SIDE)
 FACTORS = (2, STORED, CHUNKS, SIDE)
 OFFSET = (2, OFFSETS, CHUNKS, SIDE)
 
 
 def per_device(fields, material, conduct, joints_x, joints_y):
+    inputs = (fields, material, conduct, joints_x.T, joints_y.T)
     with jax.named_scope("reduce_x"):
         pay, x_factor, x_offset, y_factor, y_pay = pl.pallas_call(
             reduce_kernel,
             out_shape=(f32(*SPREAD), f32(*FACTORS), f32(*OFFSET), f32(*FACTORS), f32(ROWS, SIDE)),
-            in_specs=[VMEM, VMEM, SMEM, VMEM, VMEM],
+            in_specs=[HBM] * 5,
             out_specs=(VMEM,) * 5,
             scratch_shapes=[
                 pltpu.VMEM(BLOCK, jnp.float32),
                 pltpu.VMEM((SIDE, SIDE), jnp.int32),
+                pltpu.SMEM(conduct.shape, jnp.float32),
+                pltpu.VMEM(joints_x.shape[::-1], jnp.int32),
+                pltpu.VMEM(joints_y.shape[::-1], jnp.int32),
+                pltpu.VMEM(BLOCK, jnp.float32),
+                pltpu.VMEM((SIDE, SIDE), jnp.int32),
                 pltpu.VMEM((ROWS, SIDE), jnp.float32),
+                pltpu.SemaphoreType.DMA((5,)),
             ],
-        )(fields, material, conduct, joints_x.T, joints_y.T)
+            compiler_params=PARAMS,
+        )(*(pltpu.with_memory_space_constraint(x, pltpu.HBM) for x in inputs))
     with jax.named_scope("exchange_x"):
         gathered = lax.all_to_all(pay, "gx", 0, 0)
     with jax.named_scope("solve_x_reduce_y"):
-        half_step, pay, y_offset = pl.pallas_call(
+        half, pay, y_offset = pl.pallas_call(
             turn_kernel,
             out_shape=(f32(*BLOCK), f32(*SPREAD), f32(*OFFSET)),
             in_specs=[VMEM] * 5,
@@ -346,18 +382,23 @@
                 pltpu.VMEM(BLOCK, jnp.float32),
                 pltpu.VMEM((ROWS, SIDE), jnp.float32),
             ],
+            compiler_params=PARAMS,
         )(gathered, x_factor, x_offset, y_factor, y_pay)
     with jax.named_scope("exchange_y"):
         gathered = lax.all_to_all(pay, "gy", 0, 0)
     with jax.named_scope("solve_y"):
-        advanced = pl.pallas_call(
+        return pl.pallas_call(
             finish_kernel,
-            out_shape=f32(*BLOCK),
-            in_specs=[VMEM] * 3,
-            out_specs=VMEM,
-            scratch_shapes=[pltpu.VMEM((DEVICES * ROWS, SIDE), jnp.float32)],
-        )(gathered, y_factor, y_offset)
-    return (half_step, advanced)
+            out_shape=(f32(*BLOCK), f32(*BLOCK)),
+            in_specs=[VMEM] * 4,
+            out_specs=(HBM, HBM),
+            scratch_shapes=[
+                pltpu.VMEM((DEVICES * ROWS, SIDE), jnp.float32),
+                pltpu.VMEM(BLOCK, jnp.float32),
+                pltpu.SemaphoreType.DMA((3,)),
+            ],
+            compiler_params=PARAMS,
+        )(gathered, y_factor, y_offset, half)
 
 
 def solution(mesh):

time: 41 us -> 36.4 us (0.89)
  Pallas kernels: 6.59 us -> 2.69 us
  blocking collectives: 33.5 us -> 32.9 us
    pallas_call x1, Pallas kernels: 2.3 us -> 0.37 us  [per_device(): pl.pallas_call(turn_kernel, out_shape=(f32(*BLOCK), f32(*SPREAD), f32(*OF...]
    pallas_call x1, Pallas kernels: 1.97 us -> 0.86 us  [per_device(): pl.pallas_call(finish_kernel, out_shape=(f32(*BLOCK), f32(*BLOCK)), in_sp...]
    pallas_call x1, Pallas kernels: 2.33 us -> 1.46 us  [per_device(): pl.pallas_call(reduce_kernel, out_shape=(f32(*SPREAD), f32(*FACTORS), f32...]
where the time goes in v2:
time: 36.4 us; the launch traced here: 36.2 us
  blocking collectives  32.9 us (90%)
  Pallas kernels  2.69 us (7%)
  between operations  0.64 us (2%)
    all_to_all x1, blocking collectives, per_device(): gathered = lax.all_to_all(pay, 'gx', 0, 0)  18.9 us
    all_to_all x1, blocking collectives, per_device(): gathered = lax.all_to_all(pay, 'gy', 0, 0)  13.9 us
    pallas_call x1, Pallas kernels, per_device(): pl.pallas_call(reduce_kernel, out_shape=(f32(*SPREAD), f32(*FACTORS), f32...  1.46 us
    pallas_call x1, Pallas kernels, per_device(): pl.pallas_call(finish_kernel, out_shape=(f32(*BLOCK), f32(*BLOCK)), in_sp...  0.86 us

profile of v2, /device:TPU:1, one launch (start us, length us, event | category | flops | bytes accessed | tf_op | source)
XLA Modules:
  0.0 36.2 jit_solution(2353734984468909406)
XLA Ops:
  0.6 1.5 %reduce_x.1 = (f32[16,16,128]{2,1,0:T(8,128)S(1)}, f32[2,54,8,128]{3,2,1,0:T(8,128)S(1)}, f32[2,18,8,128]{3,2,1,0:T(8,128)S(1)}, f32[2,54,8,128]{3,2,1,0:T(8,128)S(1)}, f32[16,128]{1,0:T(8,128)S(1)}) custom-call(f32[2,128,128]{2,1,0:T(8,128)} %fields_in.1, s32[128,128]{1,0:T(8,128)} %material_in.1, f32[2,8]{1,0:T(2,128)} %conduct_in.1, s32[8,128]{1,0:T(8,128)} %bitcast.2, ...), custom_call_target="tpu_custom_call" | custom-call | tf_op jit(solution)/shard_map/reduce_x/pallas_call | solution.py:354
  2.1 18.9 %all_to_all.10.gathered_ref = f32[16,16,128]{2,1,0:T(8,128)S(1)} all-to-all(f32[16,16,128]{2,1,0:T(8,128)S(1)} %get-tuple-element.10), channel_id=1, replica_groups=mesh['gx'=16,'gy'=16] {'gx'}, dimensions={0} | all-to-all | bytes 262144 | tf_op jit(solution)/shard_map/exchange_x/all_to_all | solution.py:373
  21.0 0.4 %solve_x_reduce_y.1 = (f32[2,128,128]{2,1,0:T(8,128)S(1)}, f32[16,16,128]{2,1,0:T(8,128)S(1)}, f32[2,18,8,128]{3,2,1,0:T(8,128)S(1)}) custom-call(f32[16,16,128]{2,1,0:T(8,128)S(1)} %all_to_all.10.gathered_ref, f32[2,54,8,128]{3,2,1,0:T(8,128)S(1)} %get-tuple-element.11.x_factor_ref, f32[2,18,8,128]{3,2,1,0:T(8,128)S(1)} %get-tuple-element.12.x_offset_ref, ...), custom_call_target="tpu_custom_call" | custom-call | tf_op jit(solution)/shard_map/solve_x_reduce_y/pallas_call | solution.py:375
  21.4 13.9 %all_to_all.11.gathered_ref = f32[16,16,128]{2,1,0:T(8,128)S(1)} all-to-all(f32[16,16,128]{2,1,0:T(8,128)S(1)} %get-tuple-element.15), channel_id=1, replica_groups=mesh['gx'=16,'gy'=16] {'gy'}, dimensions={0} | all-to-all | bytes 262144 | tf_op jit(solution)/shard_map/exchange_y/all_to_all | solution.py:388
  35.4 0.9 %solve_y.1 = (f32[2,128,128]{2,1,0:T(8,128)}, f32[2,128,128]{2,1,0:T(8,128)}) custom-call(f32[16,16,128]{2,1,0:T(8,128)S(1)} %all_to_all.11.gathered_ref, f32[2,54,8,128]{3,2,1,0:T(8,128)S(1)} %get-tuple-element.13.y_factor_ref, f32[2,18,8,128]{3,2,1,0:T(8,128)S(1)} %get-tuple-element.16.y_offset_ref, f32[2,128,128]{2,1,0:T(8,128)S(1)} %get-tuple-element.17.half_ref), custom_call_target="tpu_custom_call" | custom-call | tf_op jit(solution)/shard_map/solve_y/pallas_call | solution.py:390

commit v3 on v2

--- a/solution.py
+++ b/solution.py
@@ -149,9 +149,9 @@
     return [h[k] for k in range(DEPTH)]
 
 
-def outer_ends(gathered_ref, ring_ref, me):
+def outer_ends(gathered_ref, ring_ref, me, turn):
     for d in range(DEVICES):
-        ring_ref[d * ROWS : (d + 1) * ROWS, :] = gathered_ref[lax.rem(me + 1 + d, DEVICES)]
+        ring_ref[d * ROWS : (d + 1) * ROWS, :] = gathered_ref[lax.rem(me + (1 + d - turn) % DEVICES, DEVICES)]
     own = sublane() == CHUNKS - 1
     ends = []
     for c in range(2):
@@ -293,7 +293,7 @@
     half_ref, out_ref, y_offset_ref,
     ring_ref, turned_ref, pay_ref,
 ):
-    ends = outer_ends(gathered_ref, ring_ref, lax.axis_index("gx"))
+    ends = outer_ends(gathered_ref, ring_ref, lax.axis_index("gx"), TURN_X)
     pay_ref[...] = y_pay_ref[...]
     for c in range(2):
         factors = load_factors(x_factor_ref, c, CELLS)
@@ -321,7 +321,7 @@
 ):
     copies = [pltpu.make_async_copy(half_ref, half_out, sems.at[2])]
     copies[0].start()
-    ends = outer_ends(gathered_ref, ring_ref, lax.axis_index("gy"))
+    ends = outer_ends(gathered_ref, ring_ref, lax.axis_index("gy"), TURN_Y)
     for c in range(2):
         factors = load_factors(y_factor_ref, c, CELLS)
         tree = load_factors(y_factor_ref, c, 3, 3 * CELLS)
@@ -333,6 +333,15 @@
         copies[-1].start()
     for copy in copies:
         copy.wait()
+
+
+TURN_X = 8
+TURN_Y = 10
+
+
+def turned_exchange(x, axis, turn):
+    group = [(i + turn) % DEVICES for i in range(DEVICES)]
+    return lax.all_to_all(x, axis, 0, 0, axis_index_groups=[group])
 
 
 def f32(*shape):
@@ -370,7 +379,7 @@
             compiler_params=PARAMS,
         )(*(pltpu.with_memory_space_constraint(x, pltpu.HBM) for x in inputs))
     with jax.named_scope("exchange_x"):
-        gathered = lax.all_to_all(pay, "gx", 0, 0)
+        gathered = turned_exchange(pay, "gx", TURN_X)
     with jax.named_scope("solve_x_reduce_y"):
         half, pay, y_offset = pl.pallas_call(
             turn_kernel,
@@ -385,7 +394,7 @@
             compiler_params=PARAMS,
         )(gathered, x_factor, x_offset, y_factor, y_pay)
     with jax.named_scope("exchange_y"):
-        gathered = lax.all_to_all(pay, "gy", 0, 0)
+        gathered = turned_exchange(pay, "gy", TURN_Y)
     with jax.named_scope("solve_y"):
         return pl.pallas_call(
             finish_kernel,

time: 36.4 us -> 29.9 us (0.82)
  blocking collectives: 32.9 us -> 26.3 us
    all_to_all x2, blocking collectives: 32.9 us -> 26.3 us  [turned_exchange(): return lax.all_to_all(x, axis, 0, 0, axis_index_groups=[group])]
where the time goes in v3:
time: 29.9 us; the launch traced here: 29.7 us
  blocking collectives  26.3 us (88%)
  Pallas kernels  2.69 us (9%)
  between operations  0.64 us (2%)
    all_to_all x2, blocking collectives, turned_exchange(): return lax.all_to_all(x, axis, 0, 0, axis_index_groups=[group])  26.3 us
    pallas_call x1, Pallas kernels, per_device(): pl.pallas_call(reduce_kernel, out_shape=(f32(*SPREAD), f32(*FACTORS), f32...  1.46 us
    pallas_call x1, Pallas kernels, per_device(): pl.pallas_call(finish_kernel, out_shape=(f32(*BLOCK), f32(*BLOCK)), in_sp...  0.86 us

profile of v3, /device:TPU:1, one launch (start us, length us, event | category | flops | bytes accessed | tf_op | source)
XLA Modules:
  0.0 29.7 jit_solution(1948499954650954637)
XLA Ops:
  0.6 1.5 %reduce_x.1 = (f32[16,16,128]{2,1,0:T(8,128)S(1)}, f32[2,54,8,128]{3,2,1,0:T(8,128)S(1)}, f32[2,18,8,128]{3,2,1,0:T(8,128)S(1)}, f32[2,54,8,128]{3,2,1,0:T(8,128)S(1)}, f32[16,128]{1,0:T(8,128)S(1)}) custom-call(f32[2,128,128]{2,1,0:T(8,128)} %fields_in.1, s32[128,128]{1,0:T(8,128)} %material_in.1, f32[2,8]{1,0:T(2,128)} %conduct_in.1, s32[8,128]{1,0:T(8,128)} %bitcast.2, ...), custom_call_target="tpu_custom_call" | custom-call | tf_op jit(solution)/shard_map/reduce_x/pallas_call | solution.py:363
  2.1 15.9 %all_to_all.10.gathered_ref = f32[16,16,128]{2,1,0:T(8,128)S(1)} all-to-all(f32[16,16,128]{2,1,0:T(8,128)S(1)} %get-tuple-element.10), channel_id=1, replica_groups={{128,144,160,176,192,208,224,240,0,16,32,48,64,80,96,112},{129,145,161,..., dimensions={0} | all-to-all | bytes 262144 | tf_op jit(solution)/shard_map/exchange_x/all_to_all | solution.py:344
  18.0 0.4 %solve_x_reduce_y.1 = (f32[2,128,128]{2,1,0:T(8,128)S(1)}, f32[16,16,128]{2,1,0:T(8,128)S(1)}, f32[2,18,8,128]{3,2,1,0:T(8,128)S(1)}) custom-call(f32[16,16,128]{2,1,0:T(8,128)S(1)} %all_to_all.10.gathered_ref, f32[2,54,8,128]{3,2,1,0:T(8,128)S(1)} %get-tuple-element.11.x_factor_ref, f32[2,18,8,128]{3,2,1,0:T(8,128)S(1)} %get-tuple-element.12.x_offset_ref, ...), custom_call_target="tpu_custom_call" | custom-call | tf_op jit(solution)/shard_map/solve_x_reduce_y/pallas_call | solution.py:384
  18.3 10.5 %all_to_all.11.gathered_ref = f32[16,16,128]{2,1,0:T(8,128)S(1)} all-to-all(f32[16,16,128]{2,1,0:T(8,128)S(1)} %get-tuple-element.15), channel_id=1, replica_groups={{10,11,12,13,14,15,0,1,2,3,4,5,6,7,8,9},{26,27,28,29,30,31,16,17,18,19,..., dimensions={0} | all-to-all | bytes 262144 | tf_op jit(solution)/shard_map/exchange_y/all_to_all | solution.py:344
  28.8 0.9 %solve_y.1 = (f32[2,128,128]{2,1,0:T(8,128)}, f32[2,128,128]{2,1,0:T(8,128)}) custom-call(f32[16,16,128]{2,1,0:T(8,128)S(1)} %all_to_all.11.gathered_ref, f32[2,54,8,128]{3,2,1,0:T(8,128)S(1)} %get-tuple-element.13.y_factor_ref, f32[2,18,8,128]{3,2,1,0:T(8,128)S(1)} %get-tuple-element.16.y_offset_ref, f32[2,128,128]{2,1,0:T(8,128)S(1)} %get-tuple-element.17.half_ref), custom_call_target="tpu_custom_call" | custom-call | tf_op jit(solution)/shard_map/solve_y/pallas_call | solution.py:399

commit v4 on v3

--- a/solution.py
+++ b/solution.py
@@ -335,7 +335,7 @@
         copy.wait()
 
 
-TURN_X = 8
+TURN_X = 11
 TURN_Y = 10
 
 

time: 29.9 us -> 29.3 us (0.980)
  blocking collectives: 26.3 us -> 25.7 us
    all_to_all x2, blocking collectives: 26.3 us -> 25.7 us  [turned_exchange(): return lax.all_to_all(x, axis, 0, 0, axis_index_groups=[group])]
where the time goes in v4:
time: 29.3 us; the launch traced here: 29.1 us
  blocking collectives  25.7 us (88%)
  Pallas kernels  2.69 us (9%)
  between operations  0.64 us (2%)
    all_to_all x2, blocking collectives, turned_exchange(): return lax.all_to_all(x, axis, 0, 0, axis_index_groups=[group])  25.7 us
    pallas_call x1, Pallas kernels, per_device(): pl.pallas_call(reduce_kernel, out_shape=(f32(*SPREAD), f32(*FACTORS), f32...  1.46 us
    pallas_call x1, Pallas kernels, per_device(): pl.pallas_call(finish_kernel, out_shape=(f32(*BLOCK), f32(*BLOCK)), in_sp...  0.86 us

profile of v4, /device:TPU:1, one launch (start us, length us, event | category | flops | bytes accessed | tf_op | source)
XLA Modules:
  0.0 29.1 jit_solution(15283433282488867469)
XLA Ops:
  0.6 1.5 %reduce_x.1 = (f32[16,16,128]{2,1,0:T(8,128)S(1)}, f32[2,54,8,128]{3,2,1,0:T(8,128)S(1)}, f32[2,18,8,128]{3,2,1,0:T(8,128)S(1)}, f32[2,54,8,128]{3,2,1,0:T(8,128)S(1)}, f32[16,128]{1,0:T(8,128)S(1)}) custom-call(f32[2,128,128]{2,1,0:T(8,128)} %fields_in.1, s32[128,128]{1,0:T(8,128)} %material_in.1, f32[2,8]{1,0:T(2,128)} %conduct_in.1, s32[8,128]{1,0:T(8,128)} %bitcast.2, ...), custom_call_target="tpu_custom_call" | custom-call | tf_op jit(solution)/shard_map/reduce_x/pallas_call | solution.py:363
  2.1 15.3 %all_to_all.10.gathered_ref = f32[16,16,128]{2,1,0:T(8,128)S(1)} all-to-all(f32[16,16,128]{2,1,0:T(8,128)S(1)} %get-tuple-element.10), channel_id=1, replica_groups={{176,192,208,224,240,0,16,32,48,64,80,96,112,128,144,160},{177,193,209,..., dimensions={0} | all-to-all | bytes 262144 | tf_op jit(solution)/shard_map/exchange_x/all_to_all | solution.py:344
  17.4 0.4 %solve_x_reduce_y.1 = (f32[2,128,128]{2,1,0:T(8,128)S(1)}, f32[16,16,128]{2,1,0:T(8,128)S(1)}, f32[2,18,8,128]{3,2,1,0:T(8,128)S(1)}) custom-call(f32[16,16,128]{2,1,0:T(8,128)S(1)} %all_to_all.10.gathered_ref, f32[2,54,8,128]{3,2,1,0:T(8,128)S(1)} %get-tuple-element.11.x_factor_ref, f32[2,18,8,128]{3,2,1,0:T(8,128)S(1)} %get-tuple-element.12.x_offset_ref, ...), custom_call_target="tpu_custom_call" | custom-call | tf_op jit(solution)/shard_map/solve_x_reduce_y/pallas_call | solution.py:384
  17.8 10.4 %all_to_all.11.gathered_ref = f32[16,16,128]{2,1,0:T(8,128)S(1)} all-to-all(f32[16,16,128]{2,1,0:T(8,128)S(1)} %get-tuple-element.15), channel_id=1, replica_groups={{10,11,12,13,14,15,0,1,2,3,4,5,6,7,8,9},{26,27,28,29,30,31,16,17,18,19,..., dimensions={0} | all-to-all | bytes 262144 | tf_op jit(solution)/shard_map/exchange_y/all_to_all | solution.py:344
  28.2 0.9 %solve_y.1 = (f32[2,128,128]{2,1,0:T(8,128)}, f32[2,128,128]{2,1,0:T(8,128)}) custom-call(f32[16,16,128]{2,1,0:T(8,128)S(1)} %all_to_all.11.gathered_ref, f32[2,54,8,128]{3,2,1,0:T(8,128)S(1)} %get-tuple-element.13.y_factor_ref, f32[2,18,8,128]{3,2,1,0:T(8,128)S(1)} %get-tuple-element.16.y_offset_ref, f32[2,128,128]{2,1,0:T(8,128)S(1)} %get-tuple-element.17.half_ref), custom_call_target="tpu_custom_call" | custom-call | tf_op jit(solution)/shard_map/solve_y/pallas_call | solution.py:399

commit v5 on v4

--- a/solution.py
+++ b/solution.py
@@ -15,8 +15,9 @@
 SIDE = 128
 DEVICES = 16
 ROWS = 16
-
-G_LOW, G_HIGH, LINK, S_LOW, S_HIGH, C_LOW, C_HIGH, OPEN = range(8)
+SLABS, SLAB = 3, 4
+G_LOW, G_HIGH, LINK, S_LOW, S_HIGH = range(5)
+KIND_LOW, KIND_HIGH, OPEN = 10, 11, 12
 
 
 def sublane():
@@ -27,19 +28,22 @@
     return pltpu.roll(x, shift % CHUNKS, 0)
 
 
+def chosen(kind, values):
+    for b in (1, 2, 4):
+        bit = (kind & b) != 0
+        values = [jnp.where(bit, values[i + 1], values[i]) for i in range(0, len(values), 2)]
+    return values[0]
+
+
 def conductivities(load, conduct_ref):
-    out = ([], [])
-    for k in range(DEPTH):
-        m = load(k)
-        bits = [(m & b) != 0 for b in (1, 2, 4)]
-        for c in range(2):
-            values = [conduct_ref[c, q] * HALF_SCALE[c] for q in range(MATERIALS)]
-            for bit in bits:
-                values = [
-                    jnp.where(bit, values[i + 1], values[i]) for i in range(0, len(values), 2)
-                ]
-            out[c].append(values[0])
-    return out
+    kinds = [load(k) for k in range(DEPTH)]
+    return [
+        [
+            chosen(kind, [conduct_ref[c, q] * HALF_SCALE[c] for q in range(MATERIALS)])
+            for kind in kinds
+        ]
+        for c in range(2)
+    ]
 
 
 def cut_bits(joints_ref, base):
@@ -149,28 +153,55 @@
     return [h[k] for k in range(DEPTH)]
 
 
-def outer_ends(gathered_ref, ring_ref, me, turn):
+def gates(joints_ref):
+    joints = joints_ref[...]
+    flags = jnp.ones((1, SIDE), jnp.int32)
+    for q in range(joints_ref.shape[0]):
+        joint = joints[q : q + 1, :]
+        at_edge = (joint & (SIDE - 1)) == 0
+        device = lax.shift_right_logical(joint, SIDE.bit_length() - 1) & (DEVICES - 1)
+        flags = flags | jnp.where(at_edge, jnp.left_shift(1, device), 0)
+    row = lax.broadcasted_iota(jnp.int32, (DEVICES, SIDE), 0)
+    flags = jnp.broadcast_to(flags, (DEVICES, SIDE))
+    return jnp.where((lax.shift_right_logical(flags, row) & 1) != 0, 0.0, 1.0)
+
+
+def outer_ends(gathered_ref, gates_ref, table_ref, ring_ref, me, turn):
     for d in range(DEVICES):
-        ring_ref[d * ROWS : (d + 1) * ROWS, :] = gathered_ref[lax.rem(me + (1 + d - turn) % DEVICES, DEVICES)]
+        member = lax.rem(me + (1 + d - turn) % DEVICES, DEVICES)
+        for p in range(SLABS):
+            at = d * ROWS + p * SLAB
+            ring_ref[at : at + SLAB, :] = gathered_ref[SLABS * member + p]
+        device = lax.rem(me + 1 + d, DEVICES)
+        ring_ref[d * ROWS + OPEN : d * ROWS + OPEN + 1, :] = gates_ref[pl.ds(device, 1), :]
     own = sublane() == CHUNKS - 1
+
+    def part(row, odd):
+        return ring_ref[pl.ds(odd * ROWS + row, 8, stride=2 * ROWS), :]
+
+    kinds_low, kinds_high = (
+        [part(row, odd).astype(jnp.int32) for odd in range(2)] for row in (KIND_LOW, KIND_HIGH)
+    )
     ends = []
     for c in range(2):
-
-        def part(q, odd):
-            return ring_ref[pl.ds(odd * ROWS + 8 * c + q, 8, stride=2 * ROWS), :]
-
-        def gate(odd):
-            return ring_ref[pl.ds(odd * ROWS + OPEN, 8, stride=2 * ROWS), :]
-
+        values = [
+            jnp.broadcast_to(table_ref[MATERIALS * c + q : MATERIALS * c + q + 1, :], own.shape)
+            for q in range(MATERIALS)
+        ]
+        cells_low, cells_high = (
+            [chosen(kind, values) for kind in kinds] for kinds in (kinds_low, kinds_high)
+        )
         elements, sources = [], []
         for odd in range(2):
-            before = part(C_HIGH, 0) if odd else rolled(part(C_HIGH, 1), 1)
-            entry = (before + part(C_LOW, odd)) * gate(odd)
+            before = cells_high[0] if odd else rolled(cells_high[1], 1)
+            entry = (before + cells_low[odd]) * part(OPEN, odd)
             zero = jnp.zeros_like(entry)
             factor, element = join_factor(
-                (zero, zero, entry), [part(q, odd) for q in (G_LOW, G_HIGH, LINK)]
+                (zero, zero, entry), [part(2 * q + c, odd) for q in (G_LOW, G_HIGH, LINK)]
             )
-            _, source = join_source(factor, (zero, zero), [part(q, odd) for q in (S_LOW, S_HIGH)])
+            _, source = join_source(
+                factor, (zero, zero), [part(2 * q + c, odd) for q in (S_LOW, S_HIGH)]
+            )
             if odd:
                 element = [
                     jnp.where(own, y, x) for x, y in zip(element, (zero, zero, entry))
@@ -184,7 +215,7 @@
         _, source = source_tree(factors, source)
 
         def mine(q):
-            at = (DEVICES - 1) * ROWS + 8 * c + q
+            at = (DEVICES - 1) * ROWS + 2 * q + c
             return ring_ref[at : at + 1, :]
 
         g_low = mine(G_LOW) + element[1][0:1, :]
@@ -219,29 +250,36 @@
     return [x for factor in factors for x in factor]
 
 
-def static_rows(pay_ref, c, element, cells, flags, is_first):
+def put(pay_ref, row, x):
+    pay_ref[row : row + 1, :] = x
+
+
+def static_rows(pay_ref, c, element):
     for q, x in zip((G_LOW, G_HIGH, LINK), element):
-        pay_ref[8 * c + q : 8 * c + q + 1, :] = x[0:1, :]
-    pay_ref[8 * c + C_LOW : 8 * c + C_LOW + 1, :] = cells[0][0:1, :]
-    pay_ref[8 * c + C_HIGH : 8 * c + C_HIGH + 1, :] = cells[DEPTH - 1][CHUNKS - 1 : CHUNKS, :]
-    shut = ((flags[0:1, :] & 1) != 0) | is_first
-    pay_ref[8 * c + OPEN : 8 * c + OPEN + 1, :] = jnp.where(shut, 0.0, 1.0)
+        put(pay_ref, 2 * q + c, x[0:1, :])
+
+
+def kind_rows(pay_ref, kind_ref):
+    for row, at in ((KIND_LOW, 0), (KIND_HIGH, SIDE - 1)):
+        put(pay_ref, row, kind_ref[at : at + 1, :].astype(jnp.float32))
 
 
 def source_rows(pay_ref, c, source):
     for q, x in zip((S_LOW, S_HIGH), source):
-        pay_ref[8 * c + q : 8 * c + q + 1, :] = x[0:1, :]
+        put(pay_ref, 2 * q + c, x[0:1, :])
 
 
 def spread(pay_ref, out_ref):
-    pay = pay_ref[...]
-    for d in range(DEVICES):
-        out_ref[d] = pay
+    for p in range(SLABS):
+        slab = pay_ref[p * SLAB : (p + 1) * SLAB, :]
+        for d in range(DEVICES):
+            out_ref[SLABS * d + p] = slab
 
 
 def reduce_kernel(
     fields_in, material_in, conduct_in, joints_x_in, joints_y_in,
     out_ref, x_factor_ref, x_offset_ref, y_factor_ref, y_pay_ref,
+    x_gates_ref, y_gates_ref, table_ref,
     fields_ref, material_ref, conduct_ref, joints_x_ref, joints_y_ref,
     turned_ref, kind_ref, pay_ref, sems,
 ):
@@ -254,46 +292,58 @@
                 (conduct_in, conduct_ref),
                 (joints_x_in, joints_x_ref),
                 (joints_y_in, joints_y_ref),
-                (fields_in, fields_ref),
+                (fields_in.at[0], fields_ref.at[0]),
+                (fields_in.at[1], fields_ref.at[1]),
             )
         )
     ]
     for copy in copies:
         copy.start()
-    for copy in copies:
+    for copy in copies[:4]:
         copy.wait()
     kind_ref[...] = material_ref[...].T
-    for c in range(2):
-        turned_ref[c] = fields_ref[c].T
     flags = cut_bits(joints_x_ref, at_x * SIDE)
     cells = conductivities(lambda k: kind_ref[pl.ds(k, CHUNKS, stride=DEPTH), :], conduct_ref)
-    for c in range(2):
-        factors, element = factor_chunk(face_links(cells[c], flags))
+    chunks = [factor_chunk(face_links(cells[c], flags)) for c in range(2)]
+    trees = [factor_tree(element) for _, element in chunks]
+    kind_rows(pay_ref, kind_ref)
+    for c in range(2):
+        static_rows(pay_ref, c, trees[c][1])
+        save(x_factor_ref, c, 0, flatten(chunks[c][0] + trees[c][0]))
+        copies[4 + c].wait()
+        turned_ref[c] = fields_ref[c].T
         sources = [turned_ref[c, pl.ds(k, CHUNKS, stride=DEPTH), :] for k in range(DEPTH)]
-        offsets, source = source_chunk(factors, sources)
-        tree, element = factor_tree(element)
-        tree_offsets, source = source_tree(tree, source)
-        save(x_factor_ref, c, 0, flatten(factors + tree))
+        offsets, source = source_chunk(chunks[c][0], sources)
+        tree_offsets, source = source_tree(trees[c][0], source)
         save(x_offset_ref, c, 0, offsets + tree_offsets)
-        static_rows(pay_ref, c, element, cells[c], flags, at_x == 0)
         source_rows(pay_ref, c, source)
     spread(pay_ref, out_ref)
+    x_gates_ref[...] = gates(joints_x_ref)
+    y_gates_ref[...] = gates(joints_y_ref)
+    for c in range(2):
+        for q in range(MATERIALS):
+            table_ref[MATERIALS * c + q : MATERIALS * c + q + 1, :] = jnp.full(
+                (1, SIDE), conduct_ref[c, q] * HALF_SCALE[c], jnp.float32
+            )
     flags = cut_bits(joints_y_ref, at_y * SIDE)
     cells = conductivities(lambda k: material_ref[pl.ds(k, CHUNKS, stride=DEPTH), :], conduct_ref)
     y_pay_ref[...] = jnp.zeros_like(y_pay_ref)
+    kind_rows(y_pay_ref, material_ref)
     for c in range(2):
         factors, element = factor_chunk(face_links(cells[c], flags))
         tree, element = factor_tree(element)
         save(y_factor_ref, c, 0, flatten(factors + tree))
-        static_rows(y_pay_ref, c, element, cells[c], flags, at_y == 0)
+        static_rows(y_pay_ref, c, element)
 
 
 def turn_kernel(
-    gathered_ref, x_factor_ref, x_offset_ref, y_factor_ref, y_pay_ref,
+    gathered_ref, gates_ref, table_ref, x_factor_ref, x_offset_ref, y_factor_ref, y_pay_ref,
     half_ref, out_ref, y_offset_ref,
     ring_ref, turned_ref, pay_ref,
 ):
-    ends = outer_ends(gathered_ref, ring_ref, lax.axis_index("gx"), TURN_X)
+    ends = outer_ends(
+        gathered_ref, gates_ref, table_ref, ring_ref, lax.axis_index("gx"), TURN_X
+    )
     pay_ref[...] = y_pay_ref[...]
     for c in range(2):
         factors = load_factors(x_factor_ref, c, CELLS)
@@ -315,13 +365,15 @@
 
 
 def finish_kernel(
-    gathered_ref, y_factor_ref, y_offset_ref, half_ref,
+    gathered_ref, gates_ref, table_ref, y_factor_ref, y_offset_ref, half_ref,
     half_out, advanced_out,
     ring_ref, advanced_ref, sems,
 ):
     copies = [pltpu.make_async_copy(half_ref, half_out, sems.at[2])]
     copies[0].start()
-    ends = outer_ends(gathered_ref, ring_ref, lax.axis_index("gy"), TURN_Y)
+    ends = outer_ends(
+        gathered_ref, gates_ref, table_ref, ring_ref, lax.axis_index("gy"), TURN_Y
+    )
     for c in range(2):
         factors = load_factors(y_factor_ref, c, CELLS)
         tree = load_factors(y_factor_ref, c, 3, 3 * CELLS)
@@ -341,7 +393,7 @@
 
 def turned_exchange(x, axis, turn):
     group = [(i + turn) % DEVICES for i in range(DEVICES)]
-    return lax.all_to_all(x, axis, 0, 0, axis_index_groups=[group])
+    return lax.all_to_all(x, axis, 0, 0, axis_index_groups=[group], tiled=True)
 
 
 def f32(*shape):
@@ -350,7 +402,7 @@
 
 VMEM = pl.BlockSpec(memory_space=pltpu.VMEM)
 HBM = pl.BlockSpec(memory_space=pltpu.HBM)
-SPREAD = (DEVICES, ROWS, SIDE)
+SPREAD = (DEVICES * SLABS, SLAB, SIDE)
 PARAMS = pltpu.CompilerParams(vmem_limit_bytes=8 << 20)
 BLOCK = (2, SIDE, SIDE)
 FACTORS = (2, STORED, CHUNKS, SIDE)
@@ -360,11 +412,12 @@
 def per_device(fields, material, conduct, joints_x, joints_y):
     inputs = (fields, material, conduct, joints_x.T, joints_y.T)
     with jax.named_scope("reduce_x"):
-        pay, x_factor, x_offset, y_factor, y_pay = pl.pallas_call(
+        pay, x_factor, x_offset, y_factor, y_pay, x_gates, y_gates, table = pl.pallas_call(
             reduce_kernel,
-            out_shape=(f32(*SPREAD), f32(*FACTORS), f32(*OFFSET), f32(*FACTORS), f32(ROWS, SIDE)),
+            out_shape=(f32(*SPREAD), f32(*FACTORS), f32(*OFFSET), f32(*FACTORS))
+            + (f32(ROWS, SIDE), f32(DEVICES, SIDE), f32(DEVICES, SIDE), f32(2 * MATERIALS, SIDE)),
             in_specs=[HBM] * 5,
-            out_specs=(VMEM,) * 5,
+            out_specs=(VMEM,) * 8,
             scratch_shapes=[
                 pltpu.VMEM(BLOCK, jnp.float32),
                 pltpu.VMEM((SIDE, SIDE), jnp.int32),
@@ -374,7 +427,7 @@
                 pltpu.VMEM(BLOCK, jnp.float32),
                 pltpu.VMEM((SIDE, SIDE), jnp.int32),
                 pltpu.VMEM((ROWS, SIDE), jnp.float32),
-                pltpu.SemaphoreType.DMA((5,)),
+                pltpu.SemaphoreType.DMA((6,)),
             ],
             compiler_params=PARAMS,
         )(*(pltpu.with_memory_space_constraint(x, pltpu.HBM) for x in inputs))
@@ -384,7 +437,7 @@
         half, pay, y_offset = pl.pallas_call(
             turn_kernel,
             out_shape=(f32(*BLOCK), f32(*SPREAD), f32(*OFFSET)),
-            in_specs=[VMEM] * 5,
+            in_specs=[VMEM] * 7,
             out_specs=(VMEM,) * 3,
             scratch_shapes=[
                 pltpu.VMEM((DEVICES * ROWS, SIDE), jnp.float32),
@@ -392,14 +445,14 @@
                 pltpu.VMEM((ROWS, SIDE), jnp.float32),
             ],
             compiler_params=PARAMS,
-        )(gathered, x_factor, x_offset, y_factor, y_pay)
+        )(gathered, x_gates, table, x_factor, x_offset, y_factor, y_pay)
     with jax.named_scope("exchange_y"):
         gathered = turned_exchange(pay, "gy", TURN_Y)
     with jax.named_scope("solve_y"):
         return pl.pallas_call(
             finish_kernel,
             out_shape=(f32(*BLOCK), f32(*BLOCK)),
-            in_specs=[VMEM] * 4,
+            in_specs=[VMEM] * 6,
             out_specs=(HBM, HBM),
             scratch_shapes=[
                 pltpu.VMEM((DEVICES * ROWS, SIDE), jnp.float32),
@@ -407,7 +460,7 @@
                 pltpu.SemaphoreType.DMA((3,)),
             ],
             compiler_params=PARAMS,
-        )(gathered, y_factor, y_offset, half)
+        )(gathered, y_gates, table, y_factor, y_offset, half)
 
 
 def solution(mesh):

time: 29.3 us -> 28.5 us (0.973)
  blocking collectives: 25.7 us -> 24.9 us
    all_to_all x2, blocking collectives: 25.7 us -> 24.9 us  [turned_exchange(): return lax.all_to_all(x, axis, 0, 0, axis_index_groups=[group], tiled=True)]
where the time goes in v5:
time: 28.5 us; the launch traced here: 28.3 us
  blocking collectives  24.9 us (87%)
  Pallas kernels  2.76 us (10%)
  between operations  0.64 us (2%)
    all_to_all x2, blocking collectives, turned_exchange(): return lax.all_to_all(x, axis, 0, 0, axis_index_groups=[group], tiled=True)  24.9 us
    pallas_call x1, Pallas kernels, per_device(): pl.pallas_call(reduce_kernel, out_shape=(f32(*SPREAD), f32(*FACTORS), f32...  1.52 us
    pallas_call x1, Pallas kernels, per_device(): pl.pallas_call(finish_kernel, out_shape=(f32(*BLOCK), f32(*BLOCK)), in_sp...  0.87 us

profile of v5, /device:TPU:1, one launch (start us, length us, event | category | flops | bytes accessed | tf_op | source)
XLA Modules:
  0.0 28.3 jit_solution(9005622577219783945)
XLA Ops:
  0.6 1.5 %reduce_x.1 = (f32[48,4,128]{2,1,0:T(4,128)S(1)}, f32[2,54,8,128]{3,2,1,0:T(8,128)S(1)}, f32[2,18,8,128]{3,2,1,0:T(8,128)S(1)}, f32[2,54,8,128]{3,2,1,0:T(8,128)...) custom-call(f32[2,128,128]{2,1,0:T(8,128)} %fields_in.1, ...), custom_call_target="tpu_custom_call" | custom-call | tf_op jit(solution)/shard_map/reduce_x/pallas_call | solution.py:415
  2.2 14.6 %all_to_all.10.gathered_ref = f32[48,4,128]{2,1,0:T(4,128)S(1)} all-to-all(f32[48,4,128]{2,1,0:T(4,128)S(1)} %get-tuple-element.13), channel_id=1, replica_groups={{176,192,208,224,240,0,16,32,48,64,80,96,112,128,144,160},{177,193,209,..., dimensions={0} | all-to-all | bytes 196608 | tf_op jit(solution)/shard_map/exchange_x/all_to_all | solution.py:396
  16.8 0.4 %solve_x_reduce_y.1 = (f32[2,128,128]{2,1,0:T(8,128)S(1)}, f32[48,4,128]{2,1,0:T(4,128)S(1)}, f32[2,18,8,128]{3,2,1,0:T(8,128)S(1)}) custom-call(f32[48,4,128]{2,1,0:T(4,128)S(1)} %all_to_all.10.gathered_ref, f32[16,128]{1,0:T(8,128)S(1)} %get-tuple-element.14.gates_ref, f32[16,128]{1,0:T(8,128)S(1)} %get-tuple-element.15.table_ref, ...), custom_call_target="tpu_custom_call" | custom-call | tf_op jit(solution)/shard_map/solve_x_reduce_y/pallas_call | solution.py:437
  17.1 10.3 %all_to_all.11.gathered_ref = f32[48,4,128]{2,1,0:T(4,128)S(1)} all-to-all(f32[48,4,128]{2,1,0:T(4,128)S(1)} %get-tuple-element.20), channel_id=1, replica_groups={{10,11,12,13,14,15,0,1,2,3,4,5,6,7,8,9},{26,27,28,29,30,31,16,17,18,19,..., dimensions={0} | all-to-all | bytes 196608 | tf_op jit(solution)/shard_map/exchange_y/all_to_all | solution.py:396
  27.4 0.9 %solve_y.1 = (f32[2,128,128]{2,1,0:T(8,128)}, f32[2,128,128]{2,1,0:T(8,128)}) custom-call(f32[48,4,128]{2,1,0:T(4,128)S(1)} %all_to_all.11.gathered_ref, f32[16,128]{1,0:T(8,128)S(1)} %get-tuple-element.21.gates_ref, f32[16,128]{1,0:T(8,128)S(1)} %get-tuple-element.15.table_ref, f32[2,54,8,128]{3,2,1,0:T(8,128)S(1)} %get-tuple-element.18.y_factor_ref, ...), custom_call_target="tpu_custom_call" | custom-call | tf_op jit(solution)/shard_map/solve_y/pallas_call | solution.py:452

commit v6 on v5

--- a/solution.py
+++ b/solution.py
@@ -15,7 +15,7 @@
 SIDE = 128
 DEVICES = 16
 ROWS = 16
-SLABS, SLAB = 3, 4
+SLABS, SLAB = 6, 2
 G_LOW, G_HIGH, LINK, S_LOW, S_HIGH = range(5)
 KIND_LOW, KIND_HIGH, OPEN = 10, 11, 12
 
@@ -292,8 +292,7 @@
                 (conduct_in, conduct_ref),
                 (joints_x_in, joints_x_ref),
                 (joints_y_in, joints_y_ref),
-                (fields_in.at[0], fields_ref.at[0]),
-                (fields_in.at[1], fields_ref.at[1]),
+                (fields_in, fields_ref),
             )
         )
     ]
@@ -310,7 +309,8 @@
     for c in range(2):
         static_rows(pay_ref, c, trees[c][1])
         save(x_factor_ref, c, 0, flatten(chunks[c][0] + trees[c][0]))
-        copies[4 + c].wait()
+    copies[4].wait()
+    for c in range(2):
         turned_ref[c] = fields_ref[c].T
         sources = [turned_ref[c, pl.ds(k, CHUNKS, stride=DEPTH), :] for k in range(DEPTH)]
         offsets, source = source_chunk(chunks[c][0], sources)
@@ -427,7 +427,7 @@
                 pltpu.VMEM(BLOCK, jnp.float32),
                 pltpu.VMEM((SIDE, SIDE), jnp.int32),
                 pltpu.VMEM((ROWS, SIDE), jnp.float32),
-                pltpu.SemaphoreType.DMA((6,)),
+                pltpu.SemaphoreType.DMA((5,)),
             ],
             compiler_params=PARAMS,
         )(*(pltpu.with_memory_space_constraint(x, pltpu.HBM) for x in inputs))

time: 28.5 us -> 28.4 us (level)
  no operation moved by 1% of the time
where the time goes in v6:
time: 28.4 us; the launch traced here: 28.2 us
  blocking collectives  24.9 us (88%)
  Pallas kernels  2.65 us (9%)
  between operations  0.64 us (2%)
    all_to_all x2, blocking collectives, turned_exchange(): return lax.all_to_all(x, axis, 0, 0, axis_index_groups=[group], tiled=True)  24.9 us
    pallas_call x1, Pallas kernels, per_device(): pl.pallas_call(reduce_kernel, out_shape=(f32(*SPREAD), f32(*FACTORS), f32...  1.41 us
    pallas_call x1, Pallas kernels, per_device(): pl.pallas_call(finish_kernel, out_shape=(f32(*BLOCK), f32(*BLOCK)), in_sp...  0.87 us

profile of v6, /device:TPU:1, one launch (start us, length us, event | category | flops | bytes accessed | tf_op | source)
XLA Modules:
  0.0 28.2 jit_solution(16526684042633123707)
XLA Ops:
  0.6 1.4 %reduce_x.1 = (f32[96,2,128]{2,1,0:T(2,128)S(1)}, f32[2,54,8,128]{3,2,1,0:T(8,128)S(1)}, f32[2,18,8,128]{3,2,1,0:T(8,128)S(1)}, f32[2,54,8,128]{3,2,1,0:T(8,128)...) custom-call(f32[2,128,128]{2,1,0:T(8,128)} %fields_in.1, ...), custom_call_target="tpu_custom_call" | custom-call | tf_op jit(solution)/shard_map/reduce_x/pallas_call | solution.py:415
  2.1 14.6 %all_to_all.10.gathered_ref = f32[96,2,128]{2,1,0:T(2,128)S(1)} all-to-all(f32[96,2,128]{2,1,0:T(2,128)S(1)} %get-tuple-element.13), channel_id=1, replica_groups={{176,192,208,224,240,0,16,32,48,64,80,96,112,128,144,160},{177,193,209,..., dimensions={0} | all-to-all | bytes 196608 | tf_op jit(solution)/shard_map/exchange_x/all_to_all | solution.py:396
  16.7 0.4 %solve_x_reduce_y.1 = (f32[2,128,128]{2,1,0:T(8,128)S(1)}, f32[96,2,128]{2,1,0:T(2,128)S(1)}, f32[2,18,8,128]{3,2,1,0:T(8,128)S(1)}) custom-call(f32[96,2,128]{2,1,0:T(2,128)S(1)} %all_to_all.10.gathered_ref, f32[16,128]{1,0:T(8,128)S(1)} %get-tuple-element.14.gates_ref, f32[16,128]{1,0:T(8,128)S(1)} %get-tuple-element.15.table_ref, ...), custom_call_target="tpu_custom_call" | custom-call | tf_op jit(solution)/shard_map/solve_x_reduce_y/pallas_call | solution.py:437
  17.0 10.3 %all_to_all.11.gathered_ref = f32[96,2,128]{2,1,0:T(2,128)S(1)} all-to-all(f32[96,2,128]{2,1,0:T(2,128)S(1)} %get-tuple-element.20), channel_id=1, replica_groups={{10,11,12,13,14,15,0,1,2,3,4,5,6,7,8,9},{26,27,28,29,30,31,16,17,18,19,..., dimensions={0} | all-to-all | bytes 196608 | tf_op jit(solution)/shard_map/exchange_y/all_to_all | solution.py:396
  27.3 0.9 %solve_y.1 = (f32[2,128,128]{2,1,0:T(8,128)}, f32[2,128,128]{2,1,0:T(8,128)}) custom-call(f32[96,2,128]{2,1,0:T(2,128)S(1)} %all_to_all.11.gathered_ref, f32[16,128]{1,0:T(8,128)S(1)} %get-tuple-element.21.gates_ref, f32[16,128]{1,0:T(8,128)S(1)} %get-tuple-element.15.table_ref, f32[2,54,8,128]{3,2,1,0:T(8,128)S(1)} %get-tuple-element.18.y_factor_ref, ...), custom_call_target="tpu_custom_call" | custom-call | tf_op jit(solution)/shard_map/solve_y/pallas_call | solution.py:452

commit v7 on v6

--- a/solution.py
+++ b/solution.py
@@ -35,11 +35,15 @@
     return values[0]
 
 
-def conductivities(load, conduct_ref):
+def over_chunks(row):
+    return jnp.broadcast_to(row, (CHUNKS, SIDE))
+
+
+def conductivities(load, value):
     kinds = [load(k) for k in range(DEPTH)]
     return [
         [
-            chosen(kind, [conduct_ref[c, q] * HALF_SCALE[c] for q in range(MATERIALS)])
+            chosen(kind, [value(c, q) for q in range(MATERIALS)])
             for kind in kinds
         ]
         for c in range(2)
@@ -278,12 +282,11 @@
 
 def reduce_kernel(
     fields_in, material_in, conduct_in, joints_x_in, joints_y_in,
-    out_ref, x_factor_ref, x_offset_ref, y_factor_ref, y_pay_ref,
-    x_gates_ref, y_gates_ref, table_ref,
-    fields_ref, material_ref, conduct_ref, joints_x_ref, joints_y_ref,
+    out_ref, x_factor_ref, x_offset_ref, x_gates_ref, table_ref, material_ref, joints_y_ref,
+    fields_ref, conduct_ref, joints_x_ref,
     turned_ref, kind_ref, pay_ref, sems,
 ):
-    at_x, at_y = lax.axis_index("gx"), lax.axis_index("gy")
+    at_x = lax.axis_index("gx")
     copies = [
         pltpu.make_async_copy(source, target, sems.at[i])
         for i, (source, target) in enumerate(
@@ -302,7 +305,10 @@
         copy.wait()
     kind_ref[...] = material_ref[...].T
     flags = cut_bits(joints_x_ref, at_x * SIDE)
-    cells = conductivities(lambda k: kind_ref[pl.ds(k, CHUNKS, stride=DEPTH), :], conduct_ref)
+    cells = conductivities(
+        lambda k: kind_ref[pl.ds(k, CHUNKS, stride=DEPTH), :],
+        lambda c, q: conduct_ref[c, q] * HALF_SCALE[c],
+    )
     chunks = [factor_chunk(face_links(cells[c], flags)) for c in range(2)]
     trees = [factor_tree(element) for _, element in chunks]
     kind_rows(pay_ref, kind_ref)
@@ -319,32 +325,35 @@
         source_rows(pay_ref, c, source)
     spread(pay_ref, out_ref)
     x_gates_ref[...] = gates(joints_x_ref)
-    y_gates_ref[...] = gates(joints_y_ref)
     for c in range(2):
         for q in range(MATERIALS):
             table_ref[MATERIALS * c + q : MATERIALS * c + q + 1, :] = jnp.full(
                 (1, SIDE), conduct_ref[c, q] * HALF_SCALE[c], jnp.float32
             )
-    flags = cut_bits(joints_y_ref, at_y * SIDE)
-    cells = conductivities(lambda k: material_ref[pl.ds(k, CHUNKS, stride=DEPTH), :], conduct_ref)
-    y_pay_ref[...] = jnp.zeros_like(y_pay_ref)
-    kind_rows(y_pay_ref, material_ref)
-    for c in range(2):
-        factors, element = factor_chunk(face_links(cells[c], flags))
-        tree, element = factor_tree(element)
-        save(y_factor_ref, c, 0, flatten(factors + tree))
-        static_rows(y_pay_ref, c, element)
 
 
 def turn_kernel(
-    gathered_ref, gates_ref, table_ref, x_factor_ref, x_offset_ref, y_factor_ref, y_pay_ref,
-    half_ref, out_ref, y_offset_ref,
+    gathered_ref, gates_ref, table_ref, x_factor_ref, x_offset_ref, material_ref, joints_y_ref,
+    half_ref, out_ref, y_factor_ref, y_offset_ref, y_gates_ref,
     ring_ref, turned_ref, pay_ref,
 ):
     ends = outer_ends(
         gathered_ref, gates_ref, table_ref, ring_ref, lax.axis_index("gx"), TURN_X
     )
-    pay_ref[...] = y_pay_ref[...]
+    y_gates_ref[...] = gates(joints_y_ref)
+    flags = cut_bits(joints_y_ref, lax.axis_index("gy") * SIDE)
+    cells = conductivities(
+        lambda k: material_ref[pl.ds(k, CHUNKS, stride=DEPTH), :],
+        lambda c, q: over_chunks(table_ref[MATERIALS * c + q : MATERIALS * c + q + 1, :]),
+    )
+    kind_rows(pay_ref, material_ref)
+    y_factors = []
+    for c in range(2):
+        factors, element = factor_chunk(face_links(cells[c], flags))
+        tree, element = factor_tree(element)
+        y_factors.append((factors, tree))
+        save(y_factor_ref, c, 0, flatten(factors + tree))
+        static_rows(pay_ref, c, element)
     for c in range(2):
         factors = load_factors(x_factor_ref, c, CELLS)
         tree = load_factors(x_factor_ref, c, 3, 3 * CELLS)
@@ -354,8 +363,7 @@
             turned_ref[c, pl.ds(k, CHUNKS, stride=DEPTH), :] = h
         half_ref[c] = turned_ref[c].T
     for c in range(2):
-        factors = load_factors(y_factor_ref, c, CELLS)
-        tree = load_factors(y_factor_ref, c, 3, 3 * CELLS)
+        factors, tree = y_factors[c]
         sources = [half_ref[c, pl.ds(k, CHUNKS, stride=DEPTH), :] for k in range(DEPTH)]
         offsets, source = source_chunk(factors, sources)
         tree_offsets, source = source_tree(tree, source)
@@ -396,6 +404,10 @@
     return lax.all_to_all(x, axis, 0, 0, axis_index_groups=[group], tiled=True)
 
 
+def i32(*shape):
+    return jax.ShapeDtypeStruct(shape, jnp.int32)
+
+
 def f32(*shape):
     return jax.ShapeDtypeStruct(shape, jnp.float32)
 
@@ -412,18 +424,16 @@
 def per_device(fields, material, conduct, joints_x, joints_y):
     inputs = (fields, material, conduct, joints_x.T, joints_y.T)
     with jax.named_scope("reduce_x"):
-        pay, x_factor, x_offset, y_factor, y_pay, x_gates, y_gates, table = pl.pallas_call(
+        pay, x_factor, x_offset, x_gates, table, kinds, joints = pl.pallas_call(
             reduce_kernel,
-            out_shape=(f32(*SPREAD), f32(*FACTORS), f32(*OFFSET), f32(*FACTORS))
-            + (f32(ROWS, SIDE), f32(DEVICES, SIDE), f32(DEVICES, SIDE), f32(2 * MATERIALS, SIDE)),
+            out_shape=(f32(*SPREAD), f32(*FACTORS), f32(*OFFSET), f32(DEVICES, SIDE))
+            + (f32(2 * MATERIALS, SIDE), i32(SIDE, SIDE), i32(*joints_y.shape[::-1])),
             in_specs=[HBM] * 5,
-            out_specs=(VMEM,) * 8,
+            out_specs=(VMEM,) * 7,
             scratch_shapes=[
                 pltpu.VMEM(BLOCK, jnp.float32),
-                pltpu.VMEM((SIDE, SIDE), jnp.int32),
                 pltpu.SMEM(conduct.shape, jnp.float32),
                 pltpu.VMEM(joints_x.shape[::-1], jnp.int32),
-                pltpu.VMEM(joints_y.shape[::-1], jnp.int32),
                 pltpu.VMEM(BLOCK, jnp.float32),
                 pltpu.VMEM((SIDE, SIDE), jnp.int32),
                 pltpu.VMEM((ROWS, SIDE), jnp.float32),
@@ -434,18 +444,18 @@
     with jax.named_scope("exchange_x"):
         gathered = turned_exchange(pay, "gx", TURN_X)
     with jax.named_scope("solve_x_reduce_y"):
-        half, pay, y_offset = pl.pallas_call(
+        half, pay, y_factor, y_offset, y_gates = pl.pallas_call(
             turn_kernel,
-            out_shape=(f32(*BLOCK), f32(*SPREAD), f32(*OFFSET)),
+            out_shape=(f32(*BLOCK), f32(*SPREAD), f32(*FACTORS), f32(*OFFSET), f32(DEVICES, SIDE)),
             in_specs=[VMEM] * 7,
-            out_specs=(VMEM,) * 3,
+            out_specs=(VMEM,) * 5,
             scratch_shapes=[
                 pltpu.VMEM((DEVICES * ROWS, SIDE), jnp.float32),
                 pltpu.VMEM(BLOCK, jnp.float32),
                 pltpu.VMEM((ROWS, SIDE), jnp.float32),
             ],
             compiler_params=PARAMS,
-        )(gathered, x_gates, table, x_factor, x_offset, y_factor, y_pay)
+        )(gathered, x_gates, table, x_factor, x_offset, kinds, joints)
     with jax.named_scope("exchange_y"):
         gathered = turned_exchange(pay, "gy", TURN_Y)
     with jax.named_scope("solve_y"):

time: 28.4 us -> 28.4 us (level)
  no operation moved by 1% of the time
where the time goes in v7:
time: 28.4 us; the launch traced here: 28.2 us
  blocking collectives  24.9 us (88%)
  Pallas kernels  2.69 us (9%)
  between operations  0.65 us (2%)
    all_to_all x2, blocking collectives, turned_exchange(): return lax.all_to_all(x, axis, 0, 0, axis_index_groups=[group], tiled=True)  24.9 us
    pallas_call x1, Pallas kernels, per_device(): pl.pallas_call(reduce_kernel, out_shape=(f32(*SPREAD), f32(*FACTORS), f32...  1.36 us
    pallas_call x1, Pallas kernels, per_device(): pl.pallas_call(finish_kernel, out_shape=(f32(*BLOCK), f32(*BLOCK)), in_sp...  0.87 us

profile of v7, /device:TPU:1, one launch (start us, length us, event | category | flops | bytes accessed | tf_op | source)
XLA Modules:
  0.0 28.2 jit_solution(12445998403939146968)
XLA Ops:
  0.6 1.4 %reduce_x.1 = (f32[96,2,128]{2,1,0:T(2,128)S(1)}, f32[2,54,8,128]{3,2,1,0:T(8,128)S(1)}, f32[2,18,8,128]{3,2,1,0:T(8,128)S(1)}, f32[16,128]{1,0:T(8,128)S(1)}, f...) custom-call(f32[2,128,128]{2,1,0:T(8,128)} %fields_in.1, s32[128,128]{1,0:T(8,128)} %material_in.1, ...), custom_call_target="tpu_custom_call" | custom-call | tf_op jit(solution)/shard_map/reduce_x/pallas_call | solution.py:427
  2.0 14.6 %all_to_all.10.gathered_ref = f32[96,2,128]{2,1,0:T(2,128)S(1)} all-to-all(f32[96,2,128]{2,1,0:T(2,128)S(1)} %get-tuple-element.14), channel_id=1, replica_groups={{176,192,208,224,240,0,16,32,48,64,80,96,112,128,144,160},{177,193,209,..., dimensions={0} | all-to-all | bytes 196608 | tf_op jit(solution)/shard_map/exchange_x/all_to_all | solution.py:404
  16.6 0.5 %solve_x_reduce_y.1 = (f32[2,128,128]{2,1,0:T(8,128)S(1)}, f32[96,2,128]{2,1,0:T(2,128)S(1)}, f32[2,54,8,128]{3,2,1,0:T(8,128)S(1)}, f32[2,18,8,128]{3,2,1,0:T(8,128)S(1)}, f32[16,128]{1,0:T(8,128)S(1)}) custom-call(f32[96,2,128]{2,1,0:T(2,128)S(1)} %all_to_all.10.gathered_ref, f32[16,128]{1,0:T(8,128)S(1)} %get-tuple-element.15.gates_ref, ...), custom_call_target="tpu_custom_call" | custom-call | tf_op jit(solution)/shard_map/solve_x_reduce_y/pallas_call | solution.py:447
  17.1 10.3 %all_to_all.11.gathered_ref = f32[96,2,128]{2,1,0:T(2,128)S(1)} all-to-all(f32[96,2,128]{2,1,0:T(2,128)S(1)} %get-tuple-element.21), channel_id=1, replica_groups={{10,11,12,13,14,15,0,1,2,3,4,5,6,7,8,9},{26,27,28,29,30,31,16,17,18,19,..., dimensions={0} | all-to-all | bytes 196608 | tf_op jit(solution)/shard_map/exchange_y/all_to_all | solution.py:404
  27.4 0.9 %solve_y.1 = (f32[2,128,128]{2,1,0:T(8,128)}, f32[2,128,128]{2,1,0:T(8,128)}) custom-call(f32[96,2,128]{2,1,0:T(2,128)S(1)} %all_to_all.11.gathered_ref, f32[16,128]{1,0:T(8,128)S(1)} %get-tuple-element.22.gates_ref, f32[16,128]{1,0:T(8,128)S(1)} %get-tuple-element.16.table_ref, f32[2,54,8,128]{3,2,1,0:T(8,128)S(1)} %get-tuple-element.23.y_factor_ref, ...), custom_call_target="tpu_custom_call" | custom-call | tf_op jit(solution)/shard_map/solve_y/pallas_call | solution.py:462

commit v8 on v6

--- a/solution.py
+++ b/solution.py
@@ -137,7 +137,7 @@
 
 def solve_tree(factors, offsets, low, high):
     row = sublane()
-    for step, (to_low, to_high, _), offset in reversed(list(zip((1, 2, 4), factors, offsets))):
+    for step, (to_low, to_high, *_), offset in reversed(list(zip((1, 2, 4), factors, offsets))):
         middle = offset + to_low * low + to_high * high
         upper = (row & step) != 0
         low, high = jnp.where(upper, rolled(middle, step), low), jnp.where(
@@ -148,7 +148,7 @@
 
 def solve_chunk(factors, offsets, low, high):
     h = {-1: low, DEPTH - 1: high}
-    for (m, lo, hi), (to_low, to_high, _), offset in reversed(list(zip(ORDER, factors, offsets))):
+    for (m, lo, hi), (to_low, to_high, *_), offset in reversed(list(zip(ORDER, factors, offsets))):
         h[m] = offset + to_low * h[lo] + to_high * h[hi]
     return [h[k] for k in range(DEPTH)]
 
@@ -237,13 +237,14 @@
         ref[c, at + i] = x
 
 
-def load_factors(ref, c, count, at=0):
-    return [tuple(ref[c, at + 3 * i + j] for j in range(3)) for i in range(count)]
-
-
 CELLS = len(ORDER)
-STORED = 3 * CELLS + 9
-OFFSETS = CELLS + 3
+JOINS = CELLS + 3
+
+
+def load_factors(ref, c):
+    per = ref.shape[1] // JOINS
+    factors = [tuple(ref[c, per * i + j] for j in range(per)) for i in range(JOINS)]
+    return factors[:CELLS], factors[CELLS:]
 
 
 def flatten(factors):
@@ -288,52 +289,55 @@
         pltpu.make_async_copy(source, target, sems.at[i])
         for i, (source, target) in enumerate(
             (
-                (material_in, material_ref),
-                (conduct_in, conduct_ref),
                 (joints_x_in, joints_x_ref),
                 (joints_y_in, joints_y_ref),
+                (conduct_in, conduct_ref),
+                (material_in, material_ref),
                 (fields_in, fields_ref),
             )
         )
     ]
     for copy in copies:
         copy.start()
-    for copy in copies[:4]:
+    for copy in copies[:3]:
         copy.wait()
+    flags_x, flags_y = (
+        cut_bits(ref, at * SIDE) for ref, at in ((joints_x_ref, at_x), (joints_y_ref, at_y))
+    )
+    x_gates_ref[...] = gates(joints_x_ref)
+    y_gates_ref[...] = gates(joints_y_ref)
+    for c in range(2):
+        for q in range(MATERIALS):
+            table_ref[MATERIALS * c + q : MATERIALS * c + q + 1, :] = jnp.full(
+                (1, SIDE), conduct_ref[c, q] * HALF_SCALE[c], jnp.float32
+            )
+    y_pay_ref[...] = jnp.zeros_like(y_pay_ref)
+    copies[3].wait()
     kind_ref[...] = material_ref[...].T
-    flags = cut_bits(joints_x_ref, at_x * SIDE)
+    kind_rows(y_pay_ref, material_ref)
+    cells = conductivities(lambda k: material_ref[pl.ds(k, CHUNKS, stride=DEPTH), :], conduct_ref)
+    for c in range(2):
+        factors, element = factor_chunk(face_links(cells[c], flags_y))
+        tree, element = factor_tree(element)
+        save(y_factor_ref, c, 0, flatten(factors + tree))
+        static_rows(y_pay_ref, c, element)
+    kind_rows(pay_ref, kind_ref)
     cells = conductivities(lambda k: kind_ref[pl.ds(k, CHUNKS, stride=DEPTH), :], conduct_ref)
-    chunks = [factor_chunk(face_links(cells[c], flags)) for c in range(2)]
+    chunks = [factor_chunk(face_links(cells[c], flags_x)) for c in range(2)]
     trees = [factor_tree(element) for _, element in chunks]
-    kind_rows(pay_ref, kind_ref)
     for c in range(2):
         static_rows(pay_ref, c, trees[c][1])
-        save(x_factor_ref, c, 0, flatten(chunks[c][0] + trees[c][0]))
+        save(x_factor_ref, c, 0, flatten(f[:2] for f in chunks[c][0] + trees[c][0]))
     copies[4].wait()
     for c in range(2):
         turned_ref[c] = fields_ref[c].T
+    for c in range(2):
         sources = [turned_ref[c, pl.ds(k, CHUNKS, stride=DEPTH), :] for k in range(DEPTH)]
         offsets, source = source_chunk(chunks[c][0], sources)
         tree_offsets, source = source_tree(trees[c][0], source)
         save(x_offset_ref, c, 0, offsets + tree_offsets)
         source_rows(pay_ref, c, source)
     spread(pay_ref, out_ref)
-    x_gates_ref[...] = gates(joints_x_ref)
-    y_gates_ref[...] = gates(joints_y_ref)
-    for c in range(2):
-        for q in range(MATERIALS):
-            table_ref[MATERIALS * c + q : MATERIALS * c + q + 1, :] = jnp.full(
-                (1, SIDE), conduct_ref[c, q] * HALF_SCALE[c], jnp.float32
-            )
-    flags = cut_bits(joints_y_ref, at_y * SIDE)
-    cells = conductivities(lambda k: material_ref[pl.ds(k, CHUNKS, stride=DEPTH), :], conduct_ref)
-    y_pay_ref[...] = jnp.zeros_like(y_pay_ref)
-    kind_rows(y_pay_ref, material_ref)
-    for c in range(2):
-        factors, element = factor_chunk(face_links(cells[c], flags))
-        tree, element = factor_tree(element)
-        save(y_factor_ref, c, 0, flatten(factors + tree))
-        static_rows(y_pay_ref, c, element)
 
 
 def turn_kernel(
@@ -346,16 +350,14 @@
     )
     pay_ref[...] = y_pay_ref[...]
     for c in range(2):
-        factors = load_factors(x_factor_ref, c, CELLS)
-        tree = load_factors(x_factor_ref, c, 3, 3 * CELLS)
-        offsets = [x_offset_ref[c, i] for i in range(OFFSETS)]
+        factors, tree = load_factors(x_factor_ref, c)
+        offsets = [x_offset_ref[c, i] for i in range(JOINS)]
         low, high = solve_tree(tree, offsets[CELLS:], *ends[c])
         for k, h in enumerate(solve_chunk(factors, offsets[:CELLS], low, high)):
             turned_ref[c, pl.ds(k, CHUNKS, stride=DEPTH), :] = h
         half_ref[c] = turned_ref[c].T
     for c in range(2):
-        factors = load_factors(y_factor_ref, c, CELLS)
-        tree = load_factors(y_factor_ref, c, 3, 3 * CELLS)
+        factors, tree = load_factors(y_factor_ref, c)
         sources = [half_ref[c, pl.ds(k, CHUNKS, stride=DEPTH), :] for k in range(DEPTH)]
         offsets, source = source_chunk(factors, sources)
         tree_offsets, source = source_tree(tree, source)
@@ -375,9 +377,8 @@
         gathered_ref, gates_ref, table_ref, ring_ref, lax.axis_index("gy"), TURN_Y
     )
     for c in range(2):
-        factors = load_factors(y_factor_ref, c, CELLS)
-        tree = load_factors(y_factor_ref, c, 3, 3 * CELLS)
-        offsets = [y_offset_ref[c, i] for i in range(OFFSETS)]
+        factors, tree = load_factors(y_factor_ref, c)
+        offsets = [y_offset_ref[c, i] for i in range(JOINS)]
         low, high = solve_tree(tree, offsets[CELLS:], *ends[c])
         for k, h in enumerate(solve_chunk(factors, offsets[:CELLS], low, high)):
             advanced_ref[c, pl.ds(k, CHUNKS, stride=DEPTH), :] = h
@@ -405,8 +406,9 @@
 SPREAD = (DEVICES * SLABS, SLAB, SIDE)
 PARAMS = pltpu.CompilerParams(vmem_limit_bytes=8 << 20)
 BLOCK = (2, SIDE, SIDE)
-FACTORS = (2, STORED, CHUNKS, SIDE)
-OFFSET = (2, OFFSETS, CHUNKS, SIDE)
+FACTORS_X = (2, 2 * JOINS, CHUNKS, SIDE)
+FACTORS_Y = (2, 3 * JOINS, CHUNKS, SIDE)
+OFFSET = (2, JOINS, CHUNKS, SIDE)
 
 
 def per_device(fields, material, conduct, joints_x, joints_y):
@@ -414,7 +416,7 @@
     with jax.named_scope("reduce_x"):
         pay, x_factor, x_offset, y_factor, y_pay, x_gates, y_gates, table = pl.pallas_call(
             reduce_kernel,
-            out_shape=(f32(*SPREAD), f32(*FACTORS), f32(*OFFSET), f32(*FACTORS))
+            out_shape=(f32(*SPREAD), f32(*FACTORS_X), f32(*OFFSET), f32(*FACTORS_Y))
             + (f32(ROWS, SIDE), f32(DEVICES, SIDE), f32(DEVICES, SIDE), f32(2 * MATERIALS, SIDE)),
             in_specs=[HBM] * 5,
             out_specs=(VMEM,) * 8,

time: 28.4 us -> 28.4 us (level)
  no operation moved by 1% of the time
where the time goes in v8:
time: 28.4 us; the launch traced here: 28.2 us
  blocking collectives  24.9 us (88%)
  Pallas kernels  2.68 us (9%)
  between operations  0.64 us (2%)
    all_to_all x2, blocking collectives, turned_exchange(): return lax.all_to_all(x, axis, 0, 0, axis_index_groups=[group], tiled=True)  24.9 us
    pallas_call x1, Pallas kernels, per_device(): pl.pallas_call(reduce_kernel, out_shape=(f32(*SPREAD), f32(*FACTORS_X), f...  1.44 us
    pallas_call x1, Pallas kernels, per_device(): pl.pallas_call(finish_kernel, out_shape=(f32(*BLOCK), f32(*BLOCK)), in_sp...  0.87 us

profile of v8, /device:TPU:1, one launch (start us, length us, event | category | flops | bytes accessed | tf_op | source)
XLA Modules:
  0.0 28.2 jit_solution(15691728382662935270)
XLA Ops:
  0.6 1.4 %reduce_x.1 = (f32[96,2,128]{2,1,0:T(2,128)S(1)}, f32[2,36,8,128]{3,2,1,0:T(8,128)S(1)}, f32[2,18,8,128]{3,2,1,0:T(8,128)S(1)}, f32[2,54,8,128]{3,2,1,0:T(8,128)...) custom-call(f32[2,128,128]{2,1,0:T(8,128)} %fields_in.1, ...), custom_call_target="tpu_custom_call" | custom-call | tf_op jit(solution)/shard_map/reduce_x/pallas_call | solution.py:417
  2.1 14.6 %all_to_all.10.gathered_ref = f32[96,2,128]{2,1,0:T(2,128)S(1)} all-to-all(f32[96,2,128]{2,1,0:T(2,128)S(1)} %get-tuple-element.13), channel_id=1, replica_groups={{176,192,208,224,240,0,16,32,48,64,80,96,112,128,144,160},{177,193,209,..., dimensions={0} | all-to-all | bytes 196608 | tf_op jit(solution)/shard_map/exchange_x/all_to_all | solution.py:397
  16.7 0.4 %solve_x_reduce_y.1 = (f32[2,128,128]{2,1,0:T(8,128)S(1)}, f32[96,2,128]{2,1,0:T(2,128)S(1)}, f32[2,18,8,128]{3,2,1,0:T(8,128)S(1)}) custom-call(f32[96,2,128]{2,1,0:T(2,128)S(1)} %all_to_all.10.gathered_ref, f32[16,128]{1,0:T(8,128)S(1)} %get-tuple-element.14.gates_ref, f32[16,128]{1,0:T(8,128)S(1)} %get-tuple-element.15.table_ref, ...), custom_call_target="tpu_custom_call" | custom-call | tf_op jit(solution)/shard_map/solve_x_reduce_y/pallas_call | solution.py:439
  17.1 10.3 %all_to_all.11.gathered_ref = f32[96,2,128]{2,1,0:T(2,128)S(1)} all-to-all(f32[96,2,128]{2,1,0:T(2,128)S(1)} %get-tuple-element.20), channel_id=1, replica_groups={{10,11,12,13,14,15,0,1,2,3,4,5,6,7,8,9},{26,27,28,29,30,31,16,17,18,19,..., dimensions={0} | all-to-all | bytes 196608 | tf_op jit(solution)/shard_map/exchange_y/all_to_all | solution.py:397
  27.3 0.9 %solve_y.1 = (f32[2,128,128]{2,1,0:T(8,128)}, f32[2,128,128]{2,1,0:T(8,128)}) custom-call(f32[96,2,128]{2,1,0:T(2,128)S(1)} %all_to_all.11.gathered_ref, f32[16,128]{1,0:T(8,128)S(1)} %get-tuple-element.21.gates_ref, f32[16,128]{1,0:T(8,128)S(1)} %get-tuple-element.15.table_ref, f32[2,54,8,128]{3,2,1,0:T(8,128)S(1)} %get-tuple-element.18.y_factor_ref, ...), custom_call_target="tpu_custom_call" | custom-call | tf_op jit(solution)/shard_map/solve_y/pallas_call | solution.py:454
